TPU v7x, 256 devices: a whole 4x4x8 slice. The times are simulated.
256 devices in a mesh: lat: 16 (over z_lo, y, core), mem: 16 (over x, z_hi).
Axes of the slice: x: 4, y: 4, z: 8 (z_hi: 4, z_lo: 2; z = z_hi * 2 + z_lo), core: 2. Of those that a mesh axis runs over, the one named last changes fastest.
Arguments:
- predicted_fields: bfloat16 [16, 8, 768, 1440], P('mem', None, 'lat'), may hold values from -6 to 6
- weighted_polynomial: bfloat16 [768, 768, 768], P(('lat', 'mem')), may hold values from -0.21875 to 0.21875
- truth_spectrum: float32 [768, 2, 8, 768], P(('lat', 'mem')), may hold values from -5 to 5
- field_importance: float32 [8], replicated, may hold values from 0.3 to 3
- parallels_in_zone: int32 [16], replicated, may hold values from 1 to 48, as said below
- order_of_place: int32 [768], replicated, may hold values from 0 to 767, each once
Outputs:
- field_grad: bfloat16 [16, 8, 768, 1440], P('mem', None, 'lat')
Inputs may be any that keep to these rules, and one draw needn't show every extreme that they name: Band b holds latitude rows b * 48 to b * 48 + parallels_in_zone[b] - 1 of the padded grid; the others are padding; the entries sum to 721. Slot s holds order order_of_place[s] if it is at most 720; a slot with a larger entry is empty.
All inputs are finite; a program needn't handle non-finite values.
Results may differ from a plain program's by a relative error of at most 0.0084.
Values may be sent and summed in bfloat16 or wider, within the bound.
No kernel may reach another device: no remote copies, remote signals or barrier semaphores. Data moves between devices by JAX's collectives and lax.ppermute only.
A program may use at most 64 MiB of HBM per device.

v0:
```python
import math

import jax
import jax.numpy as jnp
from jax import lax
from jax.sharding import PartitionSpec as P

LMAX = 720


EPS = 0.01


def in_blocks(value, dim, count):
    dims = value.shape
    pieces = value.reshape(*dims[:dim], count, dims[dim] // count, *dims[dim + 1 :])
    return jnp.moveaxis(pieces, dim, 0)


def in_order(pieces, dim):
    pieces = jnp.moveaxis(pieces, 0, dim)
    dims = pieces.shape
    return pieces.reshape(*dims[:dim], dims[dim] * dims[dim + 1], *dims[dim + 2 :])


def one_exchange(value, axis, axes, splits, concats):
    sizes = [lax.axis_size(a) for a in axes]
    pieces = in_blocks(value, splits[0], sizes[0])
    pieces = jnp.moveaxis(in_blocks(pieces, splits[1] + 1, sizes[1]), 0, 1)
    inside = pieces.shape[2:]
    pieces = pieces.reshape(-1, *inside)
    pieces = lax.all_to_all(pieces, axis, split_axis=0, concat_axis=0, tiled=True)
    pieces = in_order(pieces.reshape(*sizes, *inside), concats[0] + 1)
    return in_order(pieces, concats[1])


def dft_table(orders, meridian_number):
    longitude = jnp.arange(meridian_number, dtype=jnp.int32)
    product = longitude[:, None] * orders[None, :] % meridian_number
    angle = 2.0 * math.pi / meridian_number * product.astype(jnp.float32)
    inuse_markers = (orders <= LMAX).astype(jnp.float32) / math.sqrt(meridian_number)
    table = jnp.stack(
        [jnp.cos(angle) * inuse_markers[None, :], -jnp.sin(angle) * inuse_markers[None, :]], axis=2
    )
    return table.reshape(meridian_number, 2 * orders.shape[0]).astype(jnp.bfloat16)


def kernel_grad(apart):
    first = apart[:, :, 0:1]
    second = apart[:, :, 1:2]
    return apart / jnp.sqrt(first * first + second * second + EPS)


def score_grad(coeffs, observed, weight, valid_full):
    members = coeffs.shape[1]
    term = kernel_grad(coeffs - observed[:, None])

    def add_member(index, total):
        other = lax.dynamic_slice_in_dim(coeffs, index, 1, 1)
        return total + kernel_grad(coeffs - other)

    pair = lax.fori_loop(0, members, add_member, jnp.zeros_like(coeffs))
    grads = weight[None, None, None, :, None] * valid_full * (term - pair / members)
    return grads.astype(jnp.bfloat16)


def local(
    predicted_fields,
    weighted_polynomial,
    truth_spectrum,
    field_importance,
    parallels_in_zone,
    order_of_place,
):
    field_kind_total = predicted_fields.shape[1]
    parallels_here = predicted_fields.shape[2]
    meridian_number = predicted_fields.shape[3]
    slot_dev = weighted_polynomial.shape[0]
    slots = order_of_place.shape[0]
    own_rows = parallels_in_zone[lax.axis_index("lat")]
    inuse_parallels = (jnp.arange(parallels_here, dtype=jnp.int32) < own_rows).astype(jnp.bfloat16)
    zeroed_entries = predicted_fields[0] * inuse_parallels[None, :, None]
    rows = zeroed_entries.reshape(field_kind_total * parallels_here, meridian_number)
    table_forward = dft_table(order_of_place, meridian_number)
    harmonic_modes = lax.dot_general(
        table_forward, rows, (((0,), (1,)), ((), ())), preferred_element_type=jnp.float32
    )
    harmonic_modes = harmonic_modes.astype(jnp.bfloat16).reshape(
        slots, 1, 2, field_kind_total, parallels_here
    )
    gathered = one_exchange(harmonic_modes, ("lat", "mem"), ("lat", "mem"), (0, 0), (4, 1))
    coeffs = jnp.einsum(
        "smrcp,spl->smrcl", gathered, weighted_polynomial, preferred_element_type=jnp.float32
    )
    own_orders = lax.dynamic_slice_in_dim(
        order_of_place, lax.axis_index(("lat", "mem")) * slot_dev, slot_dev
    )
    degree = jnp.arange(weighted_polynomial.shape[2], dtype=jnp.int32)
    valid = ((degree[None, :] >= own_orders[:, None]) & (degree[None, :] <= LMAX)).astype(
        jnp.float32
    )
    valid_full = valid[:, None, None, None, :]
    coeffs = coeffs * valid_full
    grads = score_grad(coeffs, truth_spectrum, field_importance, valid_full)
    back = jnp.einsum(
        "smrcl,spl->smrcp", grads, weighted_polynomial, preferred_element_type=jnp.float32
    )
    back = back.astype(jnp.bfloat16)
    returned = one_exchange(back, ("mem", "lat"), ("mem", "lat"), (1, 4), (0, 0))
    table_back = dft_table(order_of_place, meridian_number)
    flat = returned.reshape(2 * slots, field_kind_total * parallels_here)
    field = lax.dot_general(
        flat, table_back, (((0,), (1,)), ((), ())), preferred_element_type=jnp.float32
    )
    field = (
        field.reshape(1, field_kind_total, parallels_here, meridian_number)
        * inuse_parallels.astype(jnp.float32)[None, None, :, None]
    )
    return field.astype(jnp.bfloat16)


def solution(mesh):
    return jax.shard_map(
        local,
        mesh=mesh,
        in_specs=(
            P("mem", None, "lat", None),
            P(("lat", "mem"), None, None),
            P(("lat", "mem"), None, None, None),
            P(),
            P(),
            P(),
        ),
        out_specs=P("mem", None, "lat", None),
        check_vma=False,
    )
```

profile of v0, /device:TPU:1, one launch (start us, length us, event | category | flops | bytes accessed | tf_op | source)
XLA Modules:
  0.0 378.0 jit_solution(12575957964747912707)
XLA Ops:
  0.8 20.3 %multiply_convert_fusion.1 = (bf16[1440,768,1]{1,0,2:T(8,128)(2,1)S(1)}, bf16[1440,768,1]{1,0,2:T(8,128)(2,1)S(1)}) fusion(f32[768]{0:T(1024)S(1)} %compare_select_fusion, s32[768]{0:T(1024)} %param.13), kind=kLoop, calls=%fused_computation.16 | loop fusion | flops 15482880 | bytes 4429824 | tf_op jit(solution)/shard_map/convert
  23.5 12.6 %copy.20 = bf16[1440,768,2]{0,2,1:T(2,128)(2,1)} copy(bf16[1440,768,2]{1,0,2:T(8,128)(2,1)} %pad_maximum_fusion) | data formatting | bytes 8847360 | tf_op jit(solution)/shard_map/stack | solution.py:42
  36.1 10.7 %convert_element_type.73 = bf16[1440,1536]{0,1:T(8,128)(2,1)} reshape(bf16[1440,768,2]{0,2,1:T(2,128)(2,1)} %copy.20) | data formatting | bytes 8847360 | tf_op jit(solution)/shard_map/convert_element_type | solution.py:45
  50.0 6.0 %convolution_convert_fusion = bf16[1536,384]{1,0:T(8,128)(2,1)} fusion(bf16[1440,1536]{0,1:T(8,128)(2,1)} %convert_element_type.73, bf16[384,1440]{1,0:T(8,128)(2,1)S(1)} %bitcast.92), kind=kOutput, calls=%fused_computation.27 | convolution fusion | flops 1699282944 | bytes 6709248 | tf_op jit(solution)/shard_map/dot_general | solution.py:85
  56.0 5.2 %reshape_reshape_reshape_reshape.3 = bf16[256,3,1,2,8,48]{5,4,3,1,0,2:T(8,128)(2,1)} reshape(bf16[1536,384]{1,0:T(8,128)(2,1)} %convolution_convert_fusion) | data formatting | bytes 2359296 | tf_op jit(solution)/shard_map/reshape;reshape;reshape;reshape | solution.py:31
  65.2 6.5 %reshape.224 = bf16[256,2,1152]{2,1,0:T(2,128)(2,1)} reshape(bf16[256,1,3,2,8,48]{5,4,3,2,1,0:T(8,128)(2,1)} %bitcast_bitcast_fusion) | data formatting | bytes 2359296
  71.8 16.5 %all-to-all-start = ((bf16[256,2,1152]{2,1,0:T(2,128)(2,1)}), bf16[256,2,1152]{2,1,0:T(2,128)(2,1)}, u32[]{:S(2)}, u32[]{:S(2)}) async-start(bf16[256,2,1152]{2,1,0:T(2,128)(2,1)} %reshape.224), calls=%async_computation | async-start | bytes 2359296 | tf_op jit(solution)/shard_map/all_to_all | solution.py:32
  89.9 32.4 %all-to-all-done = bf16[256,2,1152]{2,1,0:T(2,128)(2,1)} async-done(((bf16[256,2,1152]{2,1,0:T(2,128)(2,1)}), bf16[256,2,1152]{2,1,0:T(2,128)(2,1)}, u32[]{:S(2)}, u32[]{:S(2)}) %all-to-all-start) | async-done | bytes 1179680 | tf_op jit(solution)/shard_map/all_to_all | solution.py:32
  122.3 6.1 %reshape.225 = bf16[256,1,3,2,8,48]{5,4,3,2,1,0:T(8,128)(2,1)} reshape(bf16[256,2,1152]{2,1,0:T(2,128)(2,1)} %all-to-all-done) | data formatting | bytes 2359296
  128.4 7.3 %copy.32 = bf16[16,16,3,1,2,8,48]{6,0,5,4,1,2,3:T(8,128)(2,1)} copy(bf16[16,16,3,1,2,8,48]{6,5,4,2,1,0,3:T(8,128)(2,1)} %bitcast.87) | data formatting | bytes 2359296 | tf_op jit(solution)/shard_map/reshape | solution.py:33
  135.7 5.5 %reshape.216 = bf16[16,3,1,2,8,768]{5,4,3,0,1,2:T(8,128)(2,1)} reshape(bf16[16,3,1,2,8,16,48]{6,5,4,3,0,1,2:T(8,128)(2,1)} %bitcast.88) | data formatting | bytes 2359296 | tf_op jit(solution)/shard_map/reshape | solution.py:23
  145.8 146.4 %while.14 = (s32[]{:T(128)}, f32[3,16,2,8,768]{4,3,2,1,0:T(8,128)}, f32[3,16,2,8,768]{4,3,2,1,0:T(8,128)}, s32[]{:T(128)}, s32[]{:T(128)}) while((s32[]{:T(128)}, f32[3,16,2,8,768]{4,3,2,1,0:T(8,128)}, f32[3,16,2,8,768]{4,3,2,1,0:T(8,128)}, s32[]{:T(128)}, s32[]{:T(128)}) %tuple.35), condition=%wide.region_1.2_spmd.clone, body=%wide.region_0.1_spmd.clone.sunk | while | flops 4128771 | bytes 17694832 | solution.py:62
  158.6 4.9 %select_add_fusion.2 = f32[3,16,2,8,768]{4,3,2,1,0:T(8,128)} fusion(f32[3,16,2,8,768]{4,3,2,1,0:T(8,128)} %get-tuple-element.119, f32[3,16,8,768]{3,2,1,0:T(8,128)} %fusion.49, pred[]{:T(512)S(6)} %compare.3, f32[3,16,2,8,768]{4,3,2,1,0:T(8,128)} %get-tuple-element.125, f32[3,2,8,768]{3,2,1,0:T(8,128)} %copy-done.2), kind=kLoop, calls=%fused_computation.clone.1 | loop fusion | flops 2359296 | bytes 8404993 | tf_op jit(solution)/shard_map/while/body/eval_jaxpr/add | solution.py:60
  167.8 4.9 %select_add_fusion.2 = f32[3,16,2,8,768]{4,3,2,1,0:T(8,128)} fusion(f32[3,16,2,8,768]{4,3,2,1,0:T(8,128)} %get-tuple-element.119, f32[3,16,8,768]{3,2,1,0:T(8,128)} %fusion.49, pred[]{:T(512)S(6)} %compare.3, f32[3,16,2,8,768]{4,3,2,1,0:T(8,128)} %get-tuple-element.125, f32[3,2,8,768]{3,2,1,0:T(8,128)} %copy-done.2), kind=kLoop, calls=%fused_computation.clone.1 | loop fusion | flops 2359296 | bytes 8404993 | tf_op jit(solution)/shard_map/while/body/eval_jaxpr/add | solution.py:60
  177.0 4.9 %select_add_fusion.2 = f32[3,16,2,8,768]{4,3,2,1,0:T(8,128)} fusion(f32[3,16,2,8,768]{4,3,2,1,0:T(8,128)} %get-tuple-element.119, f32[3,16,8,768]{3,2,1,0:T(8,128)} %fusion.49, pred[]{:T(512)S(6)} %compare.3, f32[3,16,2,8,768]{4,3,2,1,0:T(8,128)} %get-tuple-element.125, f32[3,2,8,768]{3,2,1,0:T(8,128)} %copy-done.2), kind=kLoop, calls=%fused_computation.clone.1 | loop fusion | flops 2359296 | bytes 8404993 | tf_op jit(solution)/shard_map/while/body/eval_jaxpr/add | solution.py:60
  186.2 4.9 %select_add_fusion.2 = f32[3,16,2,8,768]{4,3,2,1,0:T(8,128)} fusion(f32[3,16,2,8,768]{4,3,2,1,0:T(8,128)} %get-tuple-element.119, f32[3,16,8,768]{3,2,1,0:T(8,128)} %fusion.49, pred[]{:T(512)S(6)} %compare.3, f32[3,16,2,8,768]{4,3,2,1,0:T(8,128)} %get-tuple-element.125, f32[3,2,8,768]{3,2,1,0:T(8,128)} %copy-done.2), kind=kLoop, calls=%fused_computation.clone.1 | loop fusion | flops 2359296 | bytes 8404993 | tf_op jit(solution)/shard_map/while/body/eval_jaxpr/add | solution.py:60
  195.4 4.9 %select_add_fusion.2 = f32[3,16,2,8,768]{4,3,2,1,0:T(8,128)} fusion(f32[3,16,2,8,768]{4,3,2,1,0:T(8,128)} %get-tuple-element.119, f32[3,16,8,768]{3,2,1,0:T(8,128)} %fusion.49, pred[]{:T(512)S(6)} %compare.3, f32[3,16,2,8,768]{4,3,2,1,0:T(8,128)} %get-tuple-element.125, f32[3,2,8,768]{3,2,1,0:T(8,128)} %copy-done.2), kind=kLoop, calls=%fused_computation.clone.1 | loop fusion | flops 2359296 | bytes 8404993 | tf_op jit(solution)/shard_map/while/body/eval_jaxpr/add | solution.py:60
  204.6 4.9 %select_add_fusion.2 = f32[3,16,2,8,768]{4,3,2,1,0:T(8,128)} fusion(f32[3,16,2,8,768]{4,3,2,1,0:T(8,128)} %get-tuple-element.119, f32[3,16,8,768]{3,2,1,0:T(8,128)} %fusion.49, pred[]{:T(512)S(6)} %compare.3, f32[3,16,2,8,768]{4,3,2,1,0:T(8,128)} %get-tuple-element.125, f32[3,2,8,768]{3,2,1,0:T(8,128)} %copy-done.2), kind=kLoop, calls=%fused_computation.clone.1 | loop fusion | flops 2359296 | bytes 8404993 | tf_op jit(solution)/shard_map/while/body/eval_jaxpr/add | solution.py:60
  213.8 4.9 %select_add_fusion.2 = f32[3,16,2,8,768]{4,3,2,1,0:T(8,128)} fusion(f32[3,16,2,8,768]{4,3,2,1,0:T(8,128)} %get-tuple-element.119, f32[3,16,8,768]{3,2,1,0:T(8,128)} %fusion.49, pred[]{:T(512)S(6)} %compare.3, f32[3,16,2,8,768]{4,3,2,1,0:T(8,128)} %get-tuple-element.125, f32[3,2,8,768]{3,2,1,0:T(8,128)} %copy-done.2), kind=kLoop, calls=%fused_computation.clone.1 | loop fusion | flops 2359296 | bytes 8404993 | tf_op jit(solution)/shard_map/while/body/eval_jaxpr/add | solution.py:60
  223.0 4.9 %select_add_fusion.2 = f32[3,16,2,8,768]{4,3,2,1,0:T(8,128)} fusion(f32[3,16,2,8,768]{4,3,2,1,0:T(8,128)} %get-tuple-element.119, f32[3,16,8,768]{3,2,1,0:T(8,128)} %fusion.49, pred[]{:T(512)S(6)} %compare.3, f32[3,16,2,8,768]{4,3,2,1,0:T(8,128)} %get-tuple-element.125, f32[3,2,8,768]{3,2,1,0:T(8,128)} %copy-done.2), kind=kLoop, calls=%fused_computation.clone.1 | loop fusion | flops 2359296 | bytes 8404993 | tf_op jit(solution)/shard_map/while/body/eval_jaxpr/add | solution.py:60
  232.2 4.9 %select_add_fusion.2 = f32[3,16,2,8,768]{4,3,2,1,0:T(8,128)} fusion(f32[3,16,2,8,768]{4,3,2,1,0:T(8,128)} %get-tuple-element.119, f32[3,16,8,768]{3,2,1,0:T(8,128)} %fusion.49, pred[]{:T(512)S(6)} %compare.3, f32[3,16,2,8,768]{4,3,2,1,0:T(8,128)} %get-tuple-element.125, f32[3,2,8,768]{3,2,1,0:T(8,128)} %copy-done.2), kind=kLoop, calls=%fused_computation.clone.1 | loop fusion | flops 2359296 | bytes 8404993 | tf_op jit(solution)/shard_map/while/body/eval_jaxpr/add | solution.py:60
  241.4 4.9 %select_add_fusion.2 = f32[3,16,2,8,768]{4,3,2,1,0:T(8,128)} fusion(f32[3,16,2,8,768]{4,3,2,1,0:T(8,128)} %get-tuple-element.119, f32[3,16,8,768]{3,2,1,0:T(8,128)} %fusion.49, pred[]{:T(512)S(6)} %compare.3, f32[3,16,2,8,768]{4,3,2,1,0:T(8,128)} %get-tuple-element.125, f32[3,2,8,768]{3,2,1,0:T(8,128)} %copy-done.2), kind=kLoop, calls=%fused_computation.clone.1 | loop fusion | flops 2359296 | bytes 8404993 | tf_op jit(solution)/shard_map/while/body/eval_jaxpr/add | solution.py:60
  250.6 4.9 %select_add_fusion.2 = f32[3,16,2,8,768]{4,3,2,1,0:T(8,128)} fusion(f32[3,16,2,8,768]{4,3,2,1,0:T(8,128)} %get-tuple-element.119, f32[3,16,8,768]{3,2,1,0:T(8,128)} %fusion.49, pred[]{:T(512)S(6)} %compare.3, f32[3,16,2,8,768]{4,3,2,1,0:T(8,128)} %get-tuple-element.125, f32[3,2,8,768]{3,2,1,0:T(8,128)} %copy-done.2), kind=kLoop, calls=%fused_computation.clone.1 | loop fusion | flops 2359296 | bytes 8404993 | tf_op jit(solution)/shard_map/while/body/eval_jaxpr/add | solution.py:60
  259.8 4.9 %select_add_fusion.2 = f32[3,16,2,8,768]{4,3,2,1,0:T(8,128)} fusion(f32[3,16,2,8,768]{4,3,2,1,0:T(8,128)} %get-tuple-element.119, f32[3,16,8,768]{3,2,1,0:T(8,128)} %fusion.49, pred[]{:T(512)S(6)} %compare.3, f32[3,16,2,8,768]{4,3,2,1,0:T(8,128)} %get-tuple-element.125, f32[3,2,8,768]{3,2,1,0:T(8,128)} %copy-done.2), kind=kLoop, calls=%fused_computation.clone.1 | loop fusion | flops 2359296 | bytes 8404993 | tf_op jit(solution)/shard_map/while/body/eval_jaxpr/add | solution.py:60
  269.0 4.9 %select_add_fusion.2 = f32[3,16,2,8,768]{4,3,2,1,0:T(8,128)} fusion(f32[3,16,2,8,768]{4,3,2,1,0:T(8,128)} %get-tuple-element.119, f32[3,16,8,768]{3,2,1,0:T(8,128)} %fusion.49, pred[]{:T(512)S(6)} %compare.3, f32[3,16,2,8,768]{4,3,2,1,0:T(8,128)} %get-tuple-element.125, f32[3,2,8,768]{3,2,1,0:T(8,128)} %copy-done.2), kind=kLoop, calls=%fused_computation.clone.1 | loop fusion | flops 2359296 | bytes 8404993 | tf_op jit(solution)/shard_map/while/body/eval_jaxpr/add | solution.py:60
  278.2 4.9 %select_add_fusion.2 = f32[3,16,2,8,768]{4,3,2,1,0:T(8,128)} fusion(f32[3,16,2,8,768]{4,3,2,1,0:T(8,128)} %get-tuple-element.119, f32[3,16,8,768]{3,2,1,0:T(8,128)} %fusion.49, pred[]{:T(512)S(6)} %compare.3, f32[3,16,2,8,768]{4,3,2,1,0:T(8,128)} %get-tuple-element.125, f32[3,2,8,768]{3,2,1,0:T(8,128)} %copy-done.2), kind=kLoop, calls=%fused_computation.clone.1 | loop fusion | flops 2359296 | bytes 8404993 | tf_op jit(solution)/shard_map/while/body/eval_jaxpr/add | solution.py:60
  298.4 5.8 %reshape.219 = bf16[16,3,1,2,8,16,48]{6,5,4,3,0,1,2:T(8,128)(2,1)} reshape(bf16[16,3,1,2,8,768]{5,4,3,0,1,2:T(8,128)(2,1)} %fusion.30) | data formatting | bytes 2359296 | tf_op jit(solution)/shard_map/reshape | solution.py:16
  308.6 6.5 %reshape.226 = bf16[256,2,1152]{2,1,0:T(2,128)(2,1)} reshape(bf16[256,1,3,2,8,48]{5,4,3,2,1,0:T(8,128)(2,1)} %bitcast.89) | data formatting | bytes 2359296
  315.2 39.0 %all_to_all.10 = bf16[256,2,1152]{2,1,0:T(2,128)(2,1)} all-to-all(bf16[256,2,1152]{2,1,0:T(2,128)(2,1)} %reshape.226), channel_id=1, replica_groups=mesh['lat'=16,'mem'=16] {'mem','lat'}, dimensions={0} | all-to-all | bytes 2359296 | tf_op jit(solution)/shard_map/all_to_all | solution.py:32
  354.2 6.1 %reshape.227 = bf16[256,1,3,2,8,48]{5,4,3,2,1,0:T(8,128)(2,1)} reshape(bf16[256,2,1152]{2,1,0:T(2,128)(2,1)} %all_to_all.10) | data formatting | bytes 2359296
  364.7 5.2 %reshape_reshape_reshape.3 = bf16[1536,384]{1,0:T(8,128)(2,1)} reshape(bf16[16,16,3,1,2,8,48]{6,5,4,2,1,0,3:T(8,128)(2,1)} %copy.25) | data formatting | bytes 2359296 | tf_op jit(solution)/shard_map/reshape;reshape;reshape | solution.py:111
  372.3 5.7 %fusion.21 = bf16[1,8,48,1440]{3,2,1,0:T(8,128)(2,1)} fusion(bf16[8,48,1536]{2,1,0:T(8,128)(2,1)} %bitcast.93, bf16[1440,1536]{0,1:T(8,128)(2,1)} %convert_element_type.73, f32[48]{0:T(128)S(1)} %copy-done.6), kind=kOutput, calls=%fused_computation.29 | convolution fusion | flops 1699799040 | bytes 6709440 | tf_op jit(solution)/shard_map/dot_general | solution.py:112
  (111 shorter events, 111.6 us)
Async XLA Ops:
  0.0 141.2 %copy-start = (bf16[3,768,768]{2,1,0:T(8,128)(2,1)S(1)}, bf16[3,768,768]{2,1,0:T(8,128)(2,1)}, u32[]{:S(2)}) copy-start(bf16[3,768,768]{2,1,0:T(8,128)(2,1)} %param.9) | copy-start | bytes 10616836
  36.1 10.7 %copy-start.5 = (s32[16]{0:T(128)S(1)}, s32[16]{0:T(128)}, u32[]{:S(2)}) copy-start(s32[16]{0:T(128)} %param.12) | copy-start | bytes 196
  65.2 24.0 %copy-start.4 = (f32[8]{0:T(128)S(1)}, f32[8]{0:T(128)}, u32[]{:S(2)}) copy-start(f32[8]{0:T(128)} %param.11) | copy-start | bytes 100
  71.8 50.5 %all-to-all-start = ((bf16[256,2,1152]{2,1,0:T(2,128)(2,1)}), bf16[256,2,1152]{2,1,0:T(2,128)(2,1)}, u32[]{:S(2)}, u32[]{:S(2)}) async-start(bf16[256,2,1152]{2,1,0:T(2,128)(2,1)} %reshape.224), calls=%async_computation | async-start | bytes 2359296 | tf_op jit(solution)/shard_map/all_to_all | solution.py:32
  146.8 1.9 copy-start.2
  155.2 1.9 copy-start.2
  164.4 1.9 copy-start.2
  173.6 1.9 copy-start.2
  182.8 1.9 copy-start.2
  192.0 1.9 copy-start.2
  201.2 1.9 copy-start.2
  210.4 1.9 copy-start.2
  219.6 1.9 copy-start.2
  228.8 1.9 copy-start.2
  238.0 1.9 copy-start.2
  247.2 1.9 copy-start.2
  256.4 1.9 copy-start.2
  265.6 1.9 copy-start.2
  274.8 1.9 copy-start.2
  284.0 1.9 copy-start.2
  292.2 2.4 copy-start.1
  292.2 2.4 copy-start.3
  364.7 7.6 %copy-start.6 = (f32[48]{0:T(128)S(1)}, f32[48]{0:T(128)}, u32[]{:S(2)}) copy-start(f32[48]{0:T(128)} %get-tuple-element.93) | copy-start | bytes 580
where the time goes:
time: 381 us; the launch traced here: 378 us
  other arithmetic  160 us (42%)
  local copies, waits for them, and re-layouts  109 us (29%)
  blocking collectives  39 us (10%)
  waiting for transfers between devices  32.4 us (9%)
  matrix products  20.1 us (5%)
  starting transfers between devices  16.5 us (4%)
    add x16, other arithmetic, add_member(): return total + kernel_grad(coeffs - other)  77.6 us
    all_to_all x1, blocking collectives, one_exchange(): lax.all_to_all(pieces, axis, split_axis=0, concat_axis=0, tiled=True)  39 us
    all_to_all x1, waiting for transfers between devices, one_exchange(): lax.all_to_all(pieces, axis, split_axis=0, concat_axis=0, tiled=True)  32.4 us
    sub x16, other arithmetic, add_member(): return total + kernel_grad(coeffs - other)  30.6 us
    unnamed x17, local copies, waits for them, and re-layouts  29.5 us
    div x17, other arithmetic, kernel_grad(): return apart / jnp.sqrt(first * first + second * second + EPS)  25.2 us
    another operation x1, other arithmetic  20.3 us
    all_to_all x1, starting transfers between devices, one_exchange(): lax.all_to_all(pieces, axis, split_axis=0, concat_axis=0, tiled=True)  16.5 us
  transfers between devices with their start and end apart: 1, of which 1 were waited for; matrix products, arithmetic and copies ran while one was open for 0% of the time, Pallas kernels for 0%

commit v1 on v0

v1 whole, which is shorter than its diff:
```python
import functools
import math

import jax
import jax.numpy as jnp
from jax import lax
from jax.experimental import pallas as pl
from jax.experimental.pallas import tpu as pltpu
from jax.sharding import PartitionSpec as P

LMAX = 720
EPS = 0.01
LANES = 128


def angle_tables(orders, steps, meridian_number):
    product = orders[..., None] * steps % meridian_number
    angle = 2.0 * math.pi / meridian_number * product.astype(jnp.float32)
    return jnp.cos(angle), jnp.sin(angle)


def fill_tables(coarse_ref, fine_ref, cos_ref, sin_ref):
    fine_cos, fine_sin = fine_ref[0, 0], fine_ref[0, 1]
    meridian_number = cos_ref.shape[1]
    for j in range(pl.cdiv(meridian_number, LANES)):
        wide = min(LANES, meridian_number - j * LANES)
        coarse_cos = coarse_ref[0, 0, :, j : j + 1]
        coarse_sin = coarse_ref[0, 1, :, j : j + 1]
        cosine = coarse_cos * fine_cos - coarse_sin * fine_sin
        sine = -(coarse_sin * fine_cos + coarse_cos * fine_sin)
        at = slice(j * LANES, j * LANES + wide)
        cos_ref[:, at] = cosine[:, :wide].astype(jnp.bfloat16)
        sin_ref[:, at] = sine[:, :wide].astype(jnp.bfloat16)


def forward_kernel(rows_ref, live_ref, coarse_ref, fine_ref, out_ref, cos_ref, sin_ref):
    fill_tables(coarse_ref, fine_ref, cos_ref, sin_ref)
    rows = rows_ref[...]
    width = rows.shape[0]
    for part, table in enumerate((cos_ref, sin_ref)):
        modes = lax.dot_general(
            table[...], rows, (((1,), (1,)), ((), ())), preferred_element_type=jnp.float32
        )
        out_ref[:, part * width : (part + 1) * width] = (modes * live_ref[...]).astype(jnp.bfloat16)


def inverse_kernel(own_ref, back_ref, coarse_ref, fine_ref, out_ref, cos_ref, sin_ref, total_ref):
    slot = pl.program_id(0)
    fill_tables(coarse_ref, fine_ref, cos_ref, sin_ref)
    kinds, height, meridian_number = out_ref.shape
    width = kinds * height
    term = jnp.zeros((width, meridian_number), jnp.float32)
    for part, table in enumerate((cos_ref, sin_ref)):
        term = term + lax.dot_general(
            back_ref[:, part * width : (part + 1) * width],
            table[...],
            (((0,), (0,)), ((), ())),
            preferred_element_type=jnp.float32,
        )

    @pl.when(slot == 0)
    def _():
        total_ref[...] = term

    @pl.when(slot > 0)
    def _():
        total_ref[...] += term

    @pl.when(slot == pl.num_programs(0) - 1)
    def _():
        place = lax.broadcasted_iota(jnp.int32, (height, meridian_number), 0)
        live = (place < own_ref[0]).astype(jnp.float32)
        for kind in range(kinds):
            rows = total_ref[kind * height : (kind + 1) * height, :]
            out_ref[kind] = (rows * live).astype(jnp.bfloat16)


def kernel_grad(first, second):
    scale = lax.rsqrt(first * first + second * second + EPS)
    return first * scale, second * scale


def score_kernel(
    bands, members, kinds, height,
    spec_ref, poly_ref, truth_ref, weight_ref, out_ref, modes_ref, coeff_ref,
):
    width = kinds * height
    half = kinds * members
    tiles = coeff_ref.shape[0]

    for band in range(bands):
        source = slice(band * members, (band + 1) * members)
        for part in range(2):
            for kind in range(kinds):
                row = (part * kinds + kind) * members
                at = part * width + kind * height
                modes_ref[row : row + members, band * height : (band + 1) * height] = spec_ref[
                    source, at : at + height
                ]

    poly = poly_ref[0]
    coeffs = jnp.dot(modes_ref[...], poly, preferred_element_type=jnp.float32)
    for tile in range(tiles):
        coeff_ref[tile] = coeffs[:, tile * LANES : (tile + 1) * LANES]

    def per_tile(tile, carry):
        real = [coeff_ref[tile, pl.ds(m, kinds, stride=members), :] for m in range(members)]
        imag = [coeff_ref[tile, pl.ds(half + m, kinds, stride=members), :] for m in range(members)]
        pair_real = [jnp.zeros_like(real[0]) for _ in range(members)]
        pair_imag = [jnp.zeros_like(real[0]) for _ in range(members)]
        lanes = pl.ds(pl.multiple_of(tile * LANES, LANES), LANES)
        truth_real, truth_imag = truth_ref[0, 0, :, lanes], truth_ref[0, 1, :, lanes]
        weight = weight_ref[0, :, lanes]
        for m in range(members):
            for j in range(m + 1, members):
                first, second = kernel_grad(real[m] - real[j], imag[m] - imag[j])
                pair_real[m] = pair_real[m] + first
                pair_imag[m] = pair_imag[m] + second
                pair_real[j] = pair_real[j] - first
                pair_imag[j] = pair_imag[j] - second
            first, second = kernel_grad(real[m] - truth_real, imag[m] - truth_imag)
            coeff_ref[tile, pl.ds(m, kinds, stride=members), :] = weight * (
                first - pair_real[m] * (1.0 / members)
            )
            coeff_ref[tile, pl.ds(half + m, kinds, stride=members), :] = weight * (
                second - pair_imag[m] * (1.0 / members)
            )
        return carry

    lax.fori_loop(0, tiles, per_tile, 0)

    back = jnp.zeros(modes_ref.shape, jnp.float32)
    for tile in range(tiles):
        back = back + lax.dot_general(
            coeff_ref[tile].astype(jnp.bfloat16),
            poly[:, tile * LANES : (tile + 1) * LANES],
            (((1,), (1,)), ((), ())),
            preferred_element_type=jnp.float32,
        )
    modes_ref[...] = back.astype(jnp.bfloat16)

    for band in range(bands):
        target = slice(band * members, (band + 1) * members)
        for part in range(2):
            for kind in range(kinds):
                row = (part * kinds + kind) * members
                at = part * width + kind * height
                out_ref[target, at : at + height] = modes_ref[
                    row : row + members, band * height : (band + 1) * height
                ]


def local(
    predicted_fields,
    weighted_polynomial,
    truth_spectrum,
    field_importance,
    parallels_in_zone,
    order_of_place,
):
    _, kinds, height, meridian_number = predicted_fields.shape
    slot_dev, places, degrees = weighted_polynomial.shape
    slots = order_of_place.shape[0]
    devices = slots // slot_dev
    bands, members = lax.axis_size("lat"), lax.axis_size("mem")
    width = kinds * height
    own_rows = parallels_in_zone[lax.axis_index("lat")]
    live = (jnp.arange(width, dtype=jnp.int32) % height < own_rows).astype(jnp.float32)[None, :]

    orders = order_of_place.reshape(devices, slot_dev).T
    used = (orders <= LMAX).astype(jnp.float32)[:, None, :, None] / math.sqrt(meridian_number)
    fine = jnp.stack(angle_tables(orders, jnp.arange(LANES), meridian_number), axis=1) * used
    coarse = jnp.stack(
        angle_tables(orders, LANES * jnp.arange(LANES), meridian_number), axis=1
    )
    table_specs = [
        pl.BlockSpec((1, 2, devices, LANES), lambda s: (s, 0, 0, 0)),
        pl.BlockSpec((1, 2, devices, LANES), lambda s: (s, 0, 0, 0)),
    ]
    table_scratch = [
        pltpu.VMEM((devices, meridian_number), jnp.bfloat16),
        pltpu.VMEM((devices, meridian_number), jnp.bfloat16),
    ]
    exchange_shape = jax.ShapeDtypeStruct((devices, slot_dev * 2 * width), jnp.bfloat16)
    slab = pl.BlockSpec((devices, 2 * width), lambda s: (0, s))

    rows = predicted_fields.reshape(width, meridian_number)
    modes = pl.pallas_call(
        forward_kernel,
        grid=(slot_dev,),
        in_specs=[
            pl.BlockSpec((width, meridian_number), lambda s: (0, 0)),
            pl.BlockSpec((1, width), lambda s: (0, 0)),
        ]
        + table_specs,
        out_specs=slab,
        out_shape=exchange_shape,
        scratch_shapes=table_scratch,
        name="forward_dft",
    )(rows, live, coarse, fine)
    gathered = lax.all_to_all(modes, ("lat", "mem"), split_axis=0, concat_axis=0, tiled=True)

    own_orders = lax.dynamic_slice_in_dim(
        order_of_place, lax.axis_index(("lat", "mem")) * slot_dev, slot_dev
    )
    degree = jnp.arange(degrees, dtype=jnp.int32)
    valid = ((degree[None, :] >= own_orders[:, None]) & (degree[None, :] <= LMAX)).astype(
        jnp.float32
    )
    weight = field_importance[None, :, None] * valid[:, None, :]
    back = pl.pallas_call(
        functools.partial(score_kernel, bands, members, kinds, height),
        grid=(slot_dev,),
        in_specs=[
            slab,
            pl.BlockSpec((1, places, degrees), lambda s: (s, 0, 0)),
            pl.BlockSpec((1, 2, kinds, degrees), lambda s: (s, 0, 0, 0)),
            pl.BlockSpec((1, kinds, degrees), lambda s: (s, 0, 0)),
        ],
        out_specs=slab,
        out_shape=exchange_shape,
        scratch_shapes=[
            pltpu.VMEM((2 * kinds * members, places), jnp.bfloat16),
            pltpu.VMEM((degrees // LANES, 2 * kinds * members, LANES), jnp.float32),
        ],
        name="score_gradient",
    )(gathered, weighted_polynomial, truth_spectrum, weight)
    returned = lax.all_to_all(back, ("lat", "mem"), split_axis=0, concat_axis=0, tiled=True)

    field = pl.pallas_call(
        inverse_kernel,
        grid=(slot_dev,),
        in_specs=[pl.BlockSpec(memory_space=pltpu.SMEM), slab] + table_specs,
        out_specs=pl.BlockSpec((kinds, height, meridian_number), lambda s: (0, 0, 0)),
        out_shape=jax.ShapeDtypeStruct((kinds, height, meridian_number), jnp.bfloat16),
        scratch_shapes=table_scratch + [pltpu.VMEM((width, meridian_number), jnp.float32)],
        name="inverse_dft",
    )(own_rows[None], returned, coarse, fine)
    return field[None]


def solution(mesh):
    return jax.shard_map(
        local,
        mesh=mesh,
        in_specs=(
            P("mem", None, "lat", None),
            P(("lat", "mem"), None, None),
            P(("lat", "mem"), None, None, None),
            P(),
            P(),
            P(),
        ),
        out_specs=P("mem", None, "lat", None),
        check_vma=False,
    )
```

time: 381 us -> 142 us (0.37)
  other arithmetic: 160 us -> 12 us
  local copies, waits for them, and re-layouts: 109 us -> 9.22 us
  Pallas kernels: 0 us -> 31.7 us
  matrix products: 20.1 us -> 0 us
    add x16 -> x0, other arithmetic: 77.6 us -> none  [add_member(): return total + kernel_grad(coeffs - other)]
    pallas_call x0 -> x3, Pallas kernels: none -> 31.7 us  [the longest x1 15.3 us: local(): pl.pallas_call(functools.partial(score_kernel, bands, members, kinds, hei...]
    sub x16 -> x0, other arithmetic: 30.6 us -> none  [add_member(): return total + kernel_grad(coeffs - other)]
    div x18 -> x1, other arithmetic: 26 us -> 0.02 us  [local(): (orders <= LMAX).astype(jnp.float32)[:, None, :, None]]
    unnamed x17 -> x8, local copies, waits for them, and re-layouts: 29.5 us -> 5.69 us
    another operation x3 -> x0, local copies, waits for them, and re-layouts: 23 us -> none  [the longest x1 12.6 us: dft_table(): jnp.stack([jnp.cos(angle) * inuse_markers[None, :], -jnp.sin(angle) * inu...]
    reshape x4 -> x1, local copies, waits for them, and re-layouts: 23 us -> 0.88 us  [local(): orders = order_of_place.reshape(devices, slot_dev).T]
    another operation x2 -> x1, other arithmetic: 22.6 us -> 1.38 us  [local(): jnp.stack(angle_tables(orders, LANES * jnp.arange(LANES), meridian_number...]
  transfers between devices with their start and end apart: 1 -> 1, of which waited for: 1 -> 1; matrix products, arithmetic and copies ran while one was open for 0% -> 1% of each run, Pallas kernels for 0% -> 0%
where the time goes in v1:
time: 142 us; the launch traced here: 141 us
  blocking collectives  39.6 us (28%)
  waiting for transfers between devices  33.2 us (23%)
  Pallas kernels  31.7 us (22%)
  starting transfers between devices  15.7 us (11%)
  other arithmetic  12 us (8%)
  local copies, waits for them, and re-layouts  9.22 us (6%)
    all_to_all x1, blocking collectives, local(): lax.all_to_all(back, ('lat', 'mem'), split_axis=0, concat_axis=0, tiled=T...  39.6 us
    all_to_all x1, waiting for transfers between devices, local(): lax.all_to_all(modes, ('lat', 'mem'), split_axis=0, concat_axis=0, tiled=...  33.2 us
    all_to_all x1, starting transfers between devices, local(): lax.all_to_all(modes, ('lat', 'mem'), split_axis=0, concat_axis=0, tiled=...  15.7 us
    pallas_call x1, Pallas kernels, local(): pl.pallas_call(functools.partial(score_kernel, bands, members, kinds, hei...  15.3 us
    pallas_call x1, Pallas kernels, local(): pl.pallas_call(inverse_kernel, grid=(slot_dev,), in_specs=[pl.BlockSpec(m...  8.73 us
    pallas_call x1, Pallas kernels, local(): pl.pallas_call(forward_kernel, grid=(slot_dev,), in_specs=[pl.BlockSpec((...  7.65 us
    unnamed x8, local copies, waits for them, and re-layouts  5.69 us
    cos x1, other arithmetic, angle_tables(): return (jnp.cos(angle), jnp.sin(angle))  3.3 us
  transfers between devices with their start and end apart: 1, of which 1 were waited for; matrix products, arithmetic and copies ran while one was open for 1% of the time, Pallas kernels for 0%

profile of v1, /device:TPU:1, one launch (start us, length us, event | category | flops | bytes accessed | tf_op | source)
XLA Modules:
  0.0 141.5 jit_solution(10480342306663894392)
XLA Ops:
  0.0 0.9 reshape.157
  0.9 0.1 copy.13
  1.0 0.1 copy.14
  1.1 1.2 dynamic_slice.6.own_ref
  2.3 1.2 compare_convert_fusion.live_ref
  3.5 3.3 %fusion.7 = (f32[3,1,256,128]{3,2,1,0:T(8,128)S(1)}, f32[3,1,256,128]{3,2,1,0:T(8,128)S(1)}, f32[3,1,256,128]{3,2,1,0:T(8,128)S(1)}, f32[3,1,256,128]{3,2,1,0:T(8,128)S(1)}) fusion(s32[3,256]{1,0:T(4,128)S(1)} %copy.13, s32[128]{0:T(128)S(1)} %iota_multiply_fusion), kind=kLoop, calls=%fused_computation.14 | loop fusion | flops 1769472 | bytes 1576448 | tf_op jit(solution)/shard_map/cos | solution.py:19
  6.8 1.4 pad_maximum_fusion
  8.2 7.7 %forward_dft.1 = bf16[256,2304]{1,0:T(8,128)(2,1)} custom-call(bf16[384,1440]{1,0:T(8,128)(2,1)} %bitcast.17, f32[1,384]{1,0:T(1,128)} %compare_convert_fusion.live_ref, f32[3,2,256,128]{3,2,1,0:T(8,128)} %get-tuple-element.11.coarse_ref, f32[3,2,256,128]{3,2,1,0:T(8,128)} %get-tuple-element.12.fine_ref), custom_call_target="tpu_custom_call" | custom-call | tf_op jit(solution)/shard_map/forward_dft/pallas_call | solution.py:188
  15.8 0.5 broadcast.229
  16.3 2.7 %reduce = bf16[256,2304]{1,0:T(8,128)(2,1)S(1)} reduce(bf16[256,1,2304]{2,0,1:T(8,128)(2,1)} %bitcast.13, bf16[]{:T(256)} %broadcast.229), dimensions={1}, to_apply=%copy.15.reduce_sub_computation | reduce | bytes 2359298 | tf_op jit(solution)/shard_map/all_to_all | solution.py:201
  19.0 1.2 reshape.158
  20.2 0.0 copy-start
  20.2 15.7 %all-to-all-start = ((bf16[256,2,1152]{2,1,0:T(2,128)(2,1)}), bf16[256,2,1152]{2,1,0:T(2,128)(2,1)S(1)}, u32[]{:S(2)}, u32[]{:S(2)}) async-start(bf16[256,2,1152]{2,1,0:T(2,128)(2,1)} %reshape.158), calls=%async_computation | async-start | bytes 2359296 | tf_op jit(solution)/shard_map/all_to_all | solution.py:201
  35.9 0.8 dynamic_slice.7
  36.6 0.1 fusion.15
  36.7 0.0 copy-done
  36.7 0.7 broadcast_multiply_fusion.weight_ref
  37.4 33.2 %all-to-all-done = bf16[256,2,1152]{2,1,0:T(2,128)(2,1)S(1)} async-done(((bf16[256,2,1152]{2,1,0:T(2,128)(2,1)}), bf16[256,2,1152]{2,1,0:T(2,128)(2,1)S(1)}, u32[]{:S(2)}, u32[]{:S(2)}) %all-to-all-start) | async-done | bytes 1179680 | tf_op jit(solution)/shard_map/all_to_all | solution.py:201
  70.6 1.0 reshape.159
  71.6 1.1 copy.22
  72.7 15.3 %score_gradient.1 = bf16[256,2304]{1,0:T(8,128)(2,1)} custom-call(bf16[256,2304]{1,0:T(8,128)(2,1)} %bitcast.15, bf16[3,768,768]{2,1,0:T(8,128)(2,1)} %poly_ref.1, f32[3,2,8,768]{3,2,1,0:T(8,128)} %truth_ref.1, f32[3,8,768]{2,1,0:T(8,128)} %broadcast_multiply_fusion.weight_ref), custom_call_target="tpu_custom_call" | custom-call | tf_op jit(solution)/shard_map/score_gradient/pallas_call | solution.py:211
  88.0 2.7 %reduce.1 = bf16[256,2304]{1,0:T(8,128)(2,1)S(1)} reduce(bf16[256,1,2304]{2,0,1:T(8,128)(2,1)} %bitcast.16, bf16[]{:T(256)} %broadcast.229), dimensions={1}, to_apply=%copy.16.reduce_sub_computation | reduce | bytes 2359298 | tf_op jit(solution)/shard_map/all_to_all | solution.py:228
  90.7 0.3 reshape.160
  91.0 39.6 %all_to_all.22 = bf16[256,2,1152]{2,1,0:T(2,128)(2,1)S(1)} all-to-all(bf16[256,2,1152]{2,1,0:T(2,128)(2,1)S(1)} %reshape.160), channel_id=1, replica_groups=mesh['lat'=16,'mem'=16] {'lat','mem'}, dimensions={0} | all-to-all | bytes 2359296 | tf_op jit(solution)/shard_map/all_to_all | solution.py:228
  130.6 1.0 reshape.161
  131.6 1.1 copy.21
  132.7 8.7 %inverse_dft.1 = bf16[8,48,1440]{2,1,0:T(8,128)(2,1)} custom-call(s32[1]{0:T(128)} %dynamic_slice.6.own_ref, bf16[256,2304]{1,0:T(8,128)(2,1)} %bitcast.14, f32[3,2,256,128]{3,2,1,0:T(8,128)} %get-tuple-element.11.coarse_ref, f32[3,2,256,128]{3,2,1,0:T(8,128)} %get-tuple-element.12.fine_ref), custom_call_target="tpu_custom_call" | custom-call | tf_op jit(solution)/shard_map/inverse_dft/pallas_call | solution.py:230
  (3 shorter events, 0.0 us)
Async XLA Ops:
  20.2 16.6 %copy-start = (f32[8]{0:T(128)S(1)}, f32[8]{0:T(128)}, u32[]{:S(2)}) copy-start(f32[8]{0:T(128)} %param.9) | copy-start | bytes 100
  20.2 50.4 %all-to-all-start = ((bf16[256,2,1152]{2,1,0:T(2,128)(2,1)}), bf16[256,2,1152]{2,1,0:T(2,128)(2,1)S(1)}, u32[]{:S(2)}, u32[]{:S(2)}) async-start(bf16[256,2,1152]{2,1,0:T(2,128)(2,1)} %reshape.158), calls=%async_computation | async-start | bytes 2359296 | tf_op jit(solution)/shard_map/all_to_all | solution.py:201

commit v2 on v1

--- a/solution.py
+++ b/solution.py
@@ -13,47 +13,74 @@
 LANES = 128
 
 
-def angle_tables(orders, steps, meridian_number):
-    product = orders[..., None] * steps % meridian_number
+BITS = 7
+
+
+def angle_tables(orders, meridian_number):
+    coarse_total = pl.cdiv(meridian_number, LANES)
+    rows = 8 * pl.cdiv(BITS + coarse_total, 8)
+    row = jnp.arange(rows, dtype=jnp.int32)[:, None]
+    is_bit = row < BITS
+    steps = jnp.where(is_bit, 1 << jnp.minimum(row, BITS), LANES * (row - BITS))
+    product = steps * orders[None, :] % meridian_number
     angle = 2.0 * math.pi / meridian_number * product.astype(jnp.float32)
-    return jnp.cos(angle), jnp.sin(angle)
-
-
-def fill_tables(coarse_ref, fine_ref, cos_ref, sin_ref):
-    fine_cos, fine_sin = fine_ref[0, 0], fine_ref[0, 1]
-    meridian_number = cos_ref.shape[1]
+    used = (orders <= LMAX).astype(jnp.float32)[None, :] / math.sqrt(meridian_number)
+    scale = jnp.where(is_bit, 1.0, used)
+    return jnp.cos(angle) * scale, jnp.sin(angle) * scale
+
+
+def turn(cos_a, sin_a, cos_b, sin_b):
+    return cos_a * cos_b - sin_a * sin_b, sin_a * cos_b + cos_a * sin_b
+
+
+def fill_tables(step_cos_ref, step_sin_ref, cos_ref, sin_ref):
+    step_cos, step_sin = step_cos_ref[...].T, step_sin_ref[...].T
+    slots, meridian_number = cos_ref.shape[1:]
+    lane = lax.broadcasted_iota(jnp.int32, (slots, LANES), 1)
+    fine_cos = jnp.ones((slots, LANES), jnp.float32)
+    fine_sin = jnp.zeros((slots, LANES), jnp.float32)
+    for bit in range(BITS):
+        column = slice(bit, bit + 1)
+        chosen = (lane & (1 << bit)) > 0
+        bit_cos = jnp.where(chosen, step_cos[:, column], 1.0)
+        bit_sin = jnp.where(chosen, step_sin[:, column], 0.0)
+        fine_cos, fine_sin = turn(fine_cos, fine_sin, bit_cos, bit_sin)
     for j in range(pl.cdiv(meridian_number, LANES)):
         wide = min(LANES, meridian_number - j * LANES)
-        coarse_cos = coarse_ref[0, 0, :, j : j + 1]
-        coarse_sin = coarse_ref[0, 1, :, j : j + 1]
-        cosine = coarse_cos * fine_cos - coarse_sin * fine_sin
-        sine = -(coarse_sin * fine_cos + coarse_cos * fine_sin)
+        column = slice(BITS + j, BITS + j + 1)
+        cosine, sine = turn(fine_cos, fine_sin, step_cos[:, column], step_sin[:, column])
         at = slice(j * LANES, j * LANES + wide)
-        cos_ref[:, at] = cosine[:, :wide].astype(jnp.bfloat16)
-        sin_ref[:, at] = sine[:, :wide].astype(jnp.bfloat16)
-
-
-def forward_kernel(rows_ref, live_ref, coarse_ref, fine_ref, out_ref, cos_ref, sin_ref):
-    fill_tables(coarse_ref, fine_ref, cos_ref, sin_ref)
-    rows = rows_ref[...]
-    width = rows.shape[0]
+        cos_ref[0, :, at] = cosine[:, :wide].astype(jnp.bfloat16)
+        sin_ref[0, :, at] = (-sine)[:, :wide].astype(jnp.bfloat16)
+
+
+def forward_kernel(zone_ref, rows_ref, step_cos_ref, step_sin_ref, out_ref, cos_ref, sin_ref):
+    fill_tables(step_cos_ref, step_sin_ref, cos_ref, sin_ref)
+    kinds, height, meridian_number = rows_ref.shape
+    width = kinds * height
+    rows = rows_ref[...].reshape(width, meridian_number)
+    own_rows = zone_ref[lax.axis_index("lat")]
+    place = lax.broadcasted_iota(jnp.int32, (1, width), 1)
+    for kind in range(kinds - 1, 0, -1):
+        place = jnp.where(place >= kind * height, place - kind * height, place)
+    live = (place < own_rows).astype(jnp.float32)
     for part, table in enumerate((cos_ref, sin_ref)):
         modes = lax.dot_general(
-            table[...], rows, (((1,), (1,)), ((), ())), preferred_element_type=jnp.float32
+            table[0], rows, (((1,), (1,)), ((), ())), preferred_element_type=jnp.float32
         )
-        out_ref[:, part * width : (part + 1) * width] = (modes * live_ref[...]).astype(jnp.bfloat16)
-
-
-def inverse_kernel(own_ref, back_ref, coarse_ref, fine_ref, out_ref, cos_ref, sin_ref, total_ref):
+        out_ref[:, part * width : (part + 1) * width] = (modes * live).astype(jnp.bfloat16)
+
+
+def inverse_kernel(zone_ref, back_ref, cos_ref, sin_ref, out_ref, total_ref):
     slot = pl.program_id(0)
-    fill_tables(coarse_ref, fine_ref, cos_ref, sin_ref)
     kinds, height, meridian_number = out_ref.shape
     width = kinds * height
+    own_rows = zone_ref[lax.axis_index("lat")]
     term = jnp.zeros((width, meridian_number), jnp.float32)
     for part, table in enumerate((cos_ref, sin_ref)):
         term = term + lax.dot_general(
             back_ref[:, part * width : (part + 1) * width],
-            table[...],
+            table[0],
             (((0,), (0,)), ((), ())),
             preferred_element_type=jnp.float32,
         )
@@ -69,10 +96,17 @@
     @pl.when(slot == pl.num_programs(0) - 1)
     def _():
         place = lax.broadcasted_iota(jnp.int32, (height, meridian_number), 0)
-        live = (place < own_ref[0]).astype(jnp.float32)
+        live = (place < own_rows).astype(jnp.float32)
         for kind in range(kinds):
             rows = total_ref[kind * height : (kind + 1) * height, :]
             out_ref[kind] = (rows * live).astype(jnp.bfloat16)
+
+
+def exchange(slabs):
+    devices, length = slabs.shape
+    pieces = slabs.reshape(devices, 2, length // 2)
+    pieces = lax.all_to_all(pieces, ("lat", "mem"), split_axis=0, concat_axis=0, tiled=True)
+    return pieces.reshape(devices, length)
 
 
 def kernel_grad(first, second):
@@ -164,41 +198,25 @@
     devices = slots // slot_dev
     bands, members = lax.axis_size("lat"), lax.axis_size("mem")
     width = kinds * height
-    own_rows = parallels_in_zone[lax.axis_index("lat")]
-    live = (jnp.arange(width, dtype=jnp.int32) % height < own_rows).astype(jnp.float32)[None, :]
-
-    orders = order_of_place.reshape(devices, slot_dev).T
-    used = (orders <= LMAX).astype(jnp.float32)[:, None, :, None] / math.sqrt(meridian_number)
-    fine = jnp.stack(angle_tables(orders, jnp.arange(LANES), meridian_number), axis=1) * used
-    coarse = jnp.stack(
-        angle_tables(orders, LANES * jnp.arange(LANES), meridian_number), axis=1
-    )
-    table_specs = [
-        pl.BlockSpec((1, 2, devices, LANES), lambda s: (s, 0, 0, 0)),
-        pl.BlockSpec((1, 2, devices, LANES), lambda s: (s, 0, 0, 0)),
-    ]
-    table_scratch = [
-        pltpu.VMEM((devices, meridian_number), jnp.bfloat16),
-        pltpu.VMEM((devices, meridian_number), jnp.bfloat16),
-    ]
+    orders = order_of_place.reshape(devices, slot_dev).T.reshape(slots)
+    step_cos, step_sin = angle_tables(orders, meridian_number)
+    step_spec = pl.BlockSpec((step_cos.shape[0], devices), lambda s: (0, s))
+    table_spec = pl.BlockSpec((1, devices, meridian_number), lambda s: (s, 0, 0))
+    table_shape = jax.ShapeDtypeStruct((slot_dev, devices, meridian_number), jnp.bfloat16)
+    scalars = pl.BlockSpec(memory_space=pltpu.SMEM)
     exchange_shape = jax.ShapeDtypeStruct((devices, slot_dev * 2 * width), jnp.bfloat16)
     slab = pl.BlockSpec((devices, 2 * width), lambda s: (0, s))
 
-    rows = predicted_fields.reshape(width, meridian_number)
-    modes = pl.pallas_call(
+    whole = pl.BlockSpec((kinds, height, meridian_number), lambda s: (0, 0, 0))
+    modes, table_cos, table_sin = pl.pallas_call(
         forward_kernel,
         grid=(slot_dev,),
-        in_specs=[
-            pl.BlockSpec((width, meridian_number), lambda s: (0, 0)),
-            pl.BlockSpec((1, width), lambda s: (0, 0)),
-        ]
-        + table_specs,
-        out_specs=slab,
-        out_shape=exchange_shape,
-        scratch_shapes=table_scratch,
+        in_specs=[scalars, whole, step_spec, step_spec],
+        out_specs=[slab, table_spec, table_spec],
+        out_shape=[exchange_shape, table_shape, table_shape],
         name="forward_dft",
-    )(rows, live, coarse, fine)
-    gathered = lax.all_to_all(modes, ("lat", "mem"), split_axis=0, concat_axis=0, tiled=True)
+    )(parallels_in_zone, predicted_fields[0], step_cos, step_sin)
+    gathered = exchange(modes)
 
     own_orders = lax.dynamic_slice_in_dim(
         order_of_place, lax.axis_index(("lat", "mem")) * slot_dev, slot_dev
@@ -225,17 +243,17 @@
         ],
         name="score_gradient",
     )(gathered, weighted_polynomial, truth_spectrum, weight)
-    returned = lax.all_to_all(back, ("lat", "mem"), split_axis=0, concat_axis=0, tiled=True)
+    returned = exchange(back)
 
     field = pl.pallas_call(
         inverse_kernel,
         grid=(slot_dev,),
-        in_specs=[pl.BlockSpec(memory_space=pltpu.SMEM), slab] + table_specs,
-        out_specs=pl.BlockSpec((kinds, height, meridian_number), lambda s: (0, 0, 0)),
+        in_specs=[scalars, slab, table_spec, table_spec],
+        out_specs=whole,
         out_shape=jax.ShapeDtypeStruct((kinds, height, meridian_number), jnp.bfloat16),
-        scratch_shapes=table_scratch + [pltpu.VMEM((width, meridian_number), jnp.float32)],
+        scratch_shapes=[pltpu.VMEM((width, meridian_number), jnp.float32)],
         name="inverse_dft",
-    )(own_rows[None], returned, coarse, fine)
+    )(parallels_in_zone, returned, table_cos, table_sin)
     return field[None]
 
 

time: 142 us -> 132 us (0.930)
  other arithmetic: 12 us -> 1.87 us
    reshape x1 -> x3, local copies, waits for them, and re-layouts: 0.88 us -> 7.15 us  [the longest x2 6.26 us: exchange(): pieces = slabs.reshape(devices, 2, length // 2)]
    all_to_all x2 -> x0, other arithmetic: 5.38 us -> none  [the longest x1 2.69 us: local(): lax.all_to_all(modes, ('lat', 'mem'), split_axis=0, concat_axis=0, tiled=...]
    unnamed x8 -> x4, local copies, waits for them, and re-layouts: 5.69 us -> 2.32 us
    cos x1 -> x0, other arithmetic: 3.3 us -> none  [angle_tables(): return (jnp.cos(angle), jnp.sin(angle))]
where the time goes in v2:
time: 132 us
  blocking collectives  39.6 us (30%)
  waiting for transfers between devices  33.2 us (25%)
  Pallas kernels  30.8 us (23%)
  starting transfers between devices  15.6 us (12%)
  local copies, waits for them, and re-layouts  10.3 us (8%)
  other arithmetic  1.87 us (1%)
    all_to_all x1, blocking collectives, exchange(): lax.all_to_all(pieces, ('lat', 'mem'), split_axis=0, concat_axis=0, tiled...  39.6 us
    all_to_all x1, waiting for transfers between devices, exchange(): lax.all_to_all(pieces, ('lat', 'mem'), split_axis=0, concat_axis=0, tiled...  33.2 us
    all_to_all x1, starting transfers between devices, exchange(): lax.all_to_all(pieces, ('lat', 'mem'), split_axis=0, concat_axis=0, tiled...  15.6 us
    pallas_call x1, Pallas kernels, local(): pl.pallas_call(functools.partial(score_kernel, bands, members, kinds, hei...  15.3 us
    pallas_call x1, Pallas kernels, local(): pl.pallas_call(forward_kernel, grid=(slot_dev,), in_specs=[scalars, whole...  9.46 us
    reshape x2, local copies, waits for them, and re-layouts, exchange(): pieces = slabs.reshape(devices, 2, length // 2)  6.26 us
    pallas_call x1, Pallas kernels, local(): pl.pallas_call(inverse_kernel, grid=(slot_dev,), in_specs=[scalars, slab,...  6.07 us
  transfers between devices with their start and end apart: 1, of which 1 were waited for; matrix products, arithmetic and copies ran while one was open for 1% of the time, Pallas kernels for 0%

profile of v2, /device:TPU:1, one launch (start us, length us, event | category | flops | bytes accessed | tf_op | source)
XLA Modules:
  0.0 131.5 jit_solution(2842315974192940970)
XLA Ops:
  0.0 0.9 reshape.80
  0.9 0.1 copy.7
  1.0 1.1 select_multiply_fusion
  2.1 9.5 %forward_dft.1 = (bf16[256,2304]{1,0:T(8,128)(2,1)}, bf16[3,256,1440]{2,1,0:T(8,128)(2,1)}, bf16[3,256,1440]{2,1,0:T(8,128)(2,1)}) custom-call(s32[16]{0:T(128)} %zone_ref.3, bf16[8,48,1440]{2,1,0:T(8,128)(2,1)} %bitcast.11, f32[24,768]{1,0:T(8,128)} %get-tuple-element.12.step_cos_ref, f32[24,768]{1,0:T(8,128)} %get-tuple-element.11.step_sin_ref), custom_call_target="tpu_custom_call" | custom-call | tf_op jit(solution)/shard_map/forward_dft/pallas_call | solution.py:211
  11.5 3.5 %reshape.81 = bf16[256,2,1152]{2,1,0:T(2,128)(2,1)} reshape(bf16[256,2304]{1,0:T(8,128)(2,1)} %get-tuple-element.8) | data formatting | bytes 2359296 | tf_op jit(solution)/shard_map/reshape | solution.py:107
  15.0 0.0 copy-start
  15.0 15.6 %all-to-all-start = ((bf16[256,2,1152]{2,1,0:T(2,128)(2,1)}), bf16[256,2,1152]{2,1,0:T(2,128)(2,1)S(1)}, u32[]{:S(2)}, u32[]{:S(2)}) async-start(bf16[256,2,1152]{2,1,0:T(2,128)(2,1)} %reshape.81), calls=%async_computation | async-start | bytes 2359296 | tf_op jit(solution)/shard_map/all_to_all | solution.py:108
  30.7 0.8 dynamic_slice.3
  31.5 0.1 fusion.6
  31.5 0.0 copy-done
  31.5 0.7 broadcast_multiply_fusion.weight_ref
  32.2 33.2 %all-to-all-done = bf16[256,2,1152]{2,1,0:T(2,128)(2,1)S(1)} async-done(((bf16[256,2,1152]{2,1,0:T(2,128)(2,1)}), bf16[256,2,1152]{2,1,0:T(2,128)(2,1)S(1)}, u32[]{:S(2)}, u32[]{:S(2)}) %all-to-all-start) | async-done | bytes 1179680 | tf_op jit(solution)/shard_map/all_to_all | solution.py:108
  65.4 1.1 copy.8
  66.6 15.3 %score_gradient.1 = bf16[256,2304]{1,0:T(8,128)(2,1)} custom-call(bf16[256,2304]{1,0:T(8,128)(2,1)} %bitcast.10, bf16[3,768,768]{2,1,0:T(8,128)(2,1)} %poly_ref.1, f32[3,2,8,768]{3,2,1,0:T(8,128)} %truth_ref.1, f32[3,8,768]{2,1,0:T(8,128)} %broadcast_multiply_fusion.weight_ref), custom_call_target="tpu_custom_call" | custom-call | tf_op jit(solution)/shard_map/score_gradient/pallas_call | solution.py:229
  81.9 2.8 %reshape.83 = bf16[256,2,1152]{2,1,0:T(2,128)(2,1)S(1)} reshape(bf16[256,2304]{1,0:T(8,128)(2,1)} %score_gradient.1) | data formatting | bytes 2359296 | tf_op jit(solution)/shard_map/reshape | solution.py:107
  84.7 39.6 %all_to_all.10 = bf16[256,2,1152]{2,1,0:T(2,128)(2,1)S(1)} all-to-all(bf16[256,2,1152]{2,1,0:T(2,128)(2,1)S(1)} %reshape.83), channel_id=1, replica_groups=mesh['lat'=16,'mem'=16] {'lat','mem'}, dimensions={0} | all-to-all | bytes 2359296 | tf_op jit(solution)/shard_map/all_to_all | solution.py:108
  124.3 1.2 copy.9
  125.4 6.1 %inverse_dft.1 = bf16[8,48,1440]{2,1,0:T(8,128)(2,1)} custom-call(s32[16]{0:T(128)} %zone_ref.3, bf16[256,2304]{1,0:T(8,128)(2,1)} %bitcast.7, bf16[3,256,1440]{2,1,0:T(8,128)(2,1)} %get-tuple-element.9.cos_ref, bf16[3,256,1440]{2,1,0:T(8,128)(2,1)} %get-tuple-element.10.sin_ref), custom_call_target="tpu_custom_call" | custom-call | tf_op jit(solution)/shard_map/inverse_dft/pallas_call | solution.py:248
  (5 shorter events, 0.0 us)
Async XLA Ops:
  15.0 16.5 %copy-start = (f32[8]{0:T(128)S(1)}, f32[8]{0:T(128)}, u32[]{:S(2)}) copy-start(f32[8]{0:T(128)} %param.9) | copy-start | bytes 100
  15.0 50.4 %all-to-all-start = ((bf16[256,2,1152]{2,1,0:T(2,128)(2,1)}), bf16[256,2,1152]{2,1,0:T(2,128)(2,1)S(1)}, u32[]{:S(2)}, u32[]{:S(2)}) async-start(bf16[256,2,1152]{2,1,0:T(2,128)(2,1)} %reshape.81), calls=%async_computation | async-start | bytes 2359296 | tf_op jit(solution)/shard_map/all_to_all | solution.py:108

commit v3 on v2

--- a/solution.py
+++ b/solution.py
@@ -54,8 +54,29 @@
         sin_ref[0, :, at] = (-sine)[:, :wide].astype(jnp.bfloat16)
 
 
+def fill_tables_down(step_cos_ref, step_sin_ref, cos_ref, sin_ref):
+    meridian_number, slots = cos_ref.shape
+    row = lax.broadcasted_iota(jnp.int32, (LANES, slots), 0)
+    fine_cos = jnp.ones((LANES, slots), jnp.float32)
+    fine_sin = jnp.zeros((LANES, slots), jnp.float32)
+    for bit in range(BITS):
+        at = slice(bit, bit + 1)
+        chosen = (row & (1 << bit)) > 0
+        bit_cos = jnp.where(chosen, step_cos_ref[at, :], 1.0)
+        bit_sin = jnp.where(chosen, step_sin_ref[at, :], 0.0)
+        fine_cos, fine_sin = turn(fine_cos, fine_sin, bit_cos, bit_sin)
+    for j in range(pl.cdiv(meridian_number, LANES)):
+        high = min(LANES, meridian_number - j * LANES)
+        at = slice(BITS + j, BITS + j + 1)
+        cosine, sine = turn(
+            fine_cos[:high], fine_sin[:high], step_cos_ref[at, :], step_sin_ref[at, :]
+        )
+        cos_ref[j * LANES : j * LANES + high, :] = cosine.astype(jnp.bfloat16)
+        sin_ref[j * LANES : j * LANES + high, :] = (-sine).astype(jnp.bfloat16)
+
+
 def forward_kernel(zone_ref, rows_ref, step_cos_ref, step_sin_ref, out_ref, cos_ref, sin_ref):
-    fill_tables(step_cos_ref, step_sin_ref, cos_ref, sin_ref)
+    fill_tables_down(step_cos_ref, step_sin_ref, cos_ref, sin_ref)
     kinds, height, meridian_number = rows_ref.shape
     width = kinds * height
     rows = rows_ref[...].reshape(width, meridian_number)
@@ -65,9 +86,7 @@
         place = jnp.where(place >= kind * height, place - kind * height, place)
     live = (place < own_rows).astype(jnp.float32)
     for part, table in enumerate((cos_ref, sin_ref)):
-        modes = lax.dot_general(
-            table[0], rows, (((1,), (1,)), ((), ())), preferred_element_type=jnp.float32
-        )
+        modes = jnp.dot(rows, table[...], preferred_element_type=jnp.float32).T
         out_ref[:, part * width : (part + 1) * width] = (modes * live).astype(jnp.bfloat16)
 
 
@@ -104,7 +123,9 @@
 
 def exchange(slabs):
     devices, length = slabs.shape
-    pieces = slabs.reshape(devices, 2, length // 2)
+    halves = slabs.reshape(devices // 8, 8, 2, length // 2).transpose(0, 2, 1, 3)
+    halves = lax.optimization_barrier(halves)
+    pieces = halves.transpose(0, 2, 1, 3).reshape(devices, 2, length // 2)
     pieces = lax.all_to_all(pieces, ("lat", "mem"), split_axis=0, concat_axis=0, tiled=True)
     return pieces.reshape(devices, length)
 
@@ -208,14 +229,29 @@
     slab = pl.BlockSpec((devices, 2 * width), lambda s: (0, s))
 
     whole = pl.BlockSpec((kinds, height, meridian_number), lambda s: (0, 0, 0))
-    modes, table_cos, table_sin = pl.pallas_call(
+    modes = pl.pallas_call(
         forward_kernel,
         grid=(slot_dev,),
         in_specs=[scalars, whole, step_spec, step_spec],
-        out_specs=[slab, table_spec, table_spec],
-        out_shape=[exchange_shape, table_shape, table_shape],
+        out_specs=slab,
+        out_shape=exchange_shape,
+        scratch_shapes=[pltpu.VMEM((meridian_number, devices), jnp.bfloat16)] * 2,
         name="forward_dft",
     )(parallels_in_zone, predicted_fields[0], step_cos, step_sin)
+    modes, step_cos, step_sin = lax.optimization_barrier((modes, step_cos, step_sin))
+    table_cos, table_sin = pl.pallas_call(
+        fill_tables,
+        grid=(slot_dev,),
+        in_specs=[step_spec, step_spec],
+        out_specs=[table_spec, table_spec],
+        out_shape=[table_shape, table_shape],
+        cost_estimate=pl.CostEstimate(
+            flops=8 * slots * meridian_number,
+            bytes_accessed=4 * slots * meridian_number,
+            transcendentals=0,
+        ),
+        name="inverse_tables",
+    )(step_cos, step_sin)
     gathered = exchange(modes)
 
     own_orders = lax.dynamic_slice_in_dim(

time: 132 us -> 129 us (0.977)
  blocking collectives: 39.6 us -> 0 us
  waiting for transfers between devices: 33.2 us -> 61.2 us
  starting transfers between devices: 15.6 us -> 20.8 us
  Pallas kernels: 30.8 us -> 33.7 us
    all_to_all x1 -> x0, blocking collectives: 39.6 us -> none  [exchange(): lax.all_to_all(pieces, ('lat', 'mem'), split_axis=0, concat_axis=0, tiled...]
    all_to_all x1 -> x2, waiting for transfers between devices: 33.2 us -> 61.2 us  [exchange(): lax.all_to_all(pieces, ('lat', 'mem'), split_axis=0, concat_axis=0, tiled...]
    pallas_call x0 -> x1, Pallas kernels: none -> 6.62 us  [local(): pl.pallas_call(fill_tables, grid=(slot_dev,), in_specs=[step_spec, step_s...]
    transpose x0 -> x2, local copies, waits for them, and re-layouts: none -> 6.39 us  [exchange(): pieces = halves.transpose(0, 2, 1, 3).reshape(devices, 2, length // 2)]
    reshape x2 -> x0, local copies, waits for them, and re-layouts: 6.26 us -> none  [exchange(): pieces = slabs.reshape(devices, 2, length // 2)]
    all_to_all x1 -> x2, starting transfers between devices: 15.6 us -> 20.8 us  [exchange(): lax.all_to_all(pieces, ('lat', 'mem'), split_axis=0, concat_axis=0, tiled...]
    pallas_call x1, Pallas kernels: 9.46 us -> 5.71 us  [local(): pl.pallas_call(forward_kernel, grid=(slot_dev,), in_specs=[scalars, whole...]
  transfers between devices with their start and end apart: 1 -> 2, of which waited for: 1 -> 2; matrix products, arithmetic and copies ran while one was open for 1% -> 1% of each run, Pallas kernels for 0% -> 5%
where the time goes in v3:
time: 129 us; the launch traced here: 128 us
  waiting for transfers between devices  61.2 us (47%)
  Pallas kernels  33.7 us (26%)
  starting transfers between devices  20.8 us (16%)
  local copies, waits for them, and re-layouts  10.5 us (8%)
  other arithmetic  1.87 us (1%)
    all_to_all x2, waiting for transfers between devices, exchange(): lax.all_to_all(pieces, ('lat', 'mem'), split_axis=0, concat_axis=0, tiled...  61.2 us
    all_to_all x2, starting transfers between devices, exchange(): lax.all_to_all(pieces, ('lat', 'mem'), split_axis=0, concat_axis=0, tiled...  20.8 us
    pallas_call x1, Pallas kernels, local(): pl.pallas_call(functools.partial(score_kernel, bands, members, kinds, hei...  15.3 us
    pallas_call x1, Pallas kernels, local(): pl.pallas_call(fill_tables, grid=(slot_dev,), in_specs=[step_spec, step_s...  6.62 us
    transpose x2, local copies, waits for them, and re-layouts, exchange(): pieces = halves.transpose(0, 2, 1, 3).reshape(devices, 2, length // 2)  6.39 us
    pallas_call x1, Pallas kernels, local(): pl.pallas_call(inverse_kernel, grid=(slot_dev,), in_specs=[scalars, slab,...  6.07 us
    pallas_call x1, Pallas kernels, local(): pl.pallas_call(forward_kernel, grid=(slot_dev,), in_specs=[scalars, whole...  5.71 us
  transfers between devices with their start and end apart: 2, of which 2 were waited for; matrix products, arithmetic and copies ran while one was open for 1% of the time, Pallas kernels for 5%

profile of v3, /device:TPU:1, one launch (start us, length us, event | category | flops | bytes accessed | tf_op | source)
XLA Modules:
  0.0 128.2 jit_solution(12360013425658518021)
XLA Ops:
  0.0 0.9 reshape.86
  0.9 0.1 copy.9
  1.0 1.1 select_multiply_fusion
  2.1 5.7 %forward_dft.1 = bf16[256,2304]{1,0:T(8,128)(2,1)} custom-call(s32[16]{0:T(128)} %zone_ref.3, bf16[8,48,1440]{2,1,0:T(8,128)(2,1)} %bitcast.23, f32[24,768]{1,0:T(8,128)} %get-tuple-element.11.step_cos_ref, f32[24,768]{1,0:T(8,128)} %get-tuple-element.12.step_sin_ref), custom_call_target="tpu_custom_call" | custom-call | tf_op jit(solution)/shard_map/forward_dft/pallas_call | solution.py:232
  7.8 3.2 %copy.10 = bf16[32,8,2,1152]{3,2,1,0:T(2,128)(2,1)} copy(bf16[32,8,2,1152]{3,1,2,0:T(8,128)(2,1)} %bitcast.20) | data formatting | bytes 2359296 | tf_op jit(solution)/shard_map/transpose | solution.py:128
  11.0 0.0 copy-start
  11.0 15.7 %all-to-all-start = ((bf16[256,2,1152]{2,1,0:T(2,128)(2,1)}), bf16[256,2,1152]{2,1,0:T(2,128)(2,1)S(1)}, u32[]{:S(2)}, u32[]{:S(2)}) async-start(bf16[256,2,1152]{2,1,0:T(2,128)(2,1)} %bitcast.5), calls=%async_computation | async-start | bytes 2359296 | tf_op jit(solution)/shard_map/all_to_all | solution.py:129
  26.7 0.8 dynamic_slice.3
  27.4 0.1 fusion.6
  27.5 0.0 copy-done
  27.5 0.7 broadcast_multiply_fusion.weight_ref
  28.2 33.2 %all-to-all-done = bf16[256,2,1152]{2,1,0:T(2,128)(2,1)S(1)} async-done(((bf16[256,2,1152]{2,1,0:T(2,128)(2,1)}), bf16[256,2,1152]{2,1,0:T(2,128)(2,1)S(1)}, u32[]{:S(2)}, u32[]{:S(2)}) %all-to-all-start) | async-done | bytes 1179680 | tf_op jit(solution)/shard_map/all_to_all | solution.py:129
  61.4 1.1 copy.12
  62.5 15.3 %score_gradient.1 = bf16[256,2304]{1,0:T(8,128)(2,1)} custom-call(bf16[256,2304]{1,0:T(8,128)(2,1)} %bitcast.21, bf16[3,768,768]{2,1,0:T(8,128)(2,1)} %poly_ref.1, f32[3,2,8,768]{3,2,1,0:T(8,128)} %truth_ref.1, f32[3,8,768]{2,1,0:T(8,128)} %broadcast_multiply_fusion.weight_ref), custom_call_target="tpu_custom_call" | custom-call | tf_op jit(solution)/shard_map/score_gradient/pallas_call | solution.py:265
  77.9 3.2 %copy.11 = bf16[32,8,2,1152]{3,2,1,0:T(2,128)(2,1)} copy(bf16[32,8,2,1152]{3,1,2,0:T(8,128)(2,1)} %bitcast.22) | data formatting | bytes 2359296 | tf_op jit(solution)/shard_map/transpose | solution.py:128
  81.1 5.2 %all-to-all-start.1 = ((bf16[256,2,1152]{2,1,0:T(2,128)(2,1)}), bf16[256,2,1152]{2,1,0:T(2,128)(2,1)S(1)}, u32[]{:S(2)}, u32[]{:S(2)}) async-start(bf16[256,2,1152]{2,1,0:T(2,128)(2,1)} %bitcast.9), calls=%async_computation.1 | async-start | bytes 2359296 | tf_op jit(solution)/shard_map/all_to_all | solution.py:129
  86.2 6.6 %inverse_tables.1 = (bf16[3,256,1440]{2,1,0:T(8,128)(2,1)}, bf16[3,256,1440]{2,1,0:T(8,128)(2,1)}) custom-call(f32[24,768]{1,0:T(8,128)} %get-tuple-element.11.step_cos_ref, f32[24,768]{1,0:T(8,128)} %get-tuple-element.12.step_sin_ref), custom_call_target="tpu_custom_call" | custom-call | flops 8847360 | bytes 4423680 | tf_op jit(solution)/shard_map/inverse_tables/pallas_call | solution.py:242
  92.9 28.0 %all-to-all-done.1 = bf16[256,2,1152]{2,1,0:T(2,128)(2,1)S(1)} async-done(((bf16[256,2,1152]{2,1,0:T(2,128)(2,1)}), bf16[256,2,1152]{2,1,0:T(2,128)(2,1)S(1)}, u32[]{:S(2)}, u32[]{:S(2)}) %all-to-all-start.1) | async-done | bytes 1179680 | tf_op jit(solution)/shard_map/all_to_all | solution.py:129
  120.9 1.2 copy.13
  122.1 6.1 %inverse_dft.1 = bf16[8,48,1440]{2,1,0:T(8,128)(2,1)} custom-call(s32[16]{0:T(128)} %zone_ref.3, bf16[256,2304]{1,0:T(8,128)(2,1)} %bitcast.17, bf16[3,256,1440]{2,1,0:T(8,128)(2,1)} %get-tuple-element.13.cos_ref, bf16[3,256,1440]{2,1,0:T(8,128)(2,1)} %get-tuple-element.14.sin_ref), custom_call_target="tpu_custom_call" | custom-call | tf_op jit(solution)/shard_map/inverse_dft/pallas_call | solution.py:284
  (5 shorter events, 0.0 us)
Async XLA Ops:
  11.0 16.5 %copy-start = (f32[8]{0:T(128)S(1)}, f32[8]{0:T(128)}, u32[]{:S(2)}) copy-start(f32[8]{0:T(128)} %param.9) | copy-start | bytes 100
  11.0 50.4 %all-to-all-start = ((bf16[256,2,1152]{2,1,0:T(2,128)(2,1)}), bf16[256,2,1152]{2,1,0:T(2,128)(2,1)S(1)}, u32[]{:S(2)}, u32[]{:S(2)}) async-start(bf16[256,2,1152]{2,1,0:T(2,128)(2,1)} %bitcast.5), calls=%async_computation | async-start | bytes 2359296 | tf_op jit(solution)/shard_map/all_to_all | solution.py:129
  81.1 39.8 %all-to-all-start.1 = ((bf16[256,2,1152]{2,1,0:T(2,128)(2,1)}), bf16[256,2,1152]{2,1,0:T(2,128)(2,1)S(1)}, u32[]{:S(2)}, u32[]{:S(2)}) async-start(bf16[256,2,1152]{2,1,0:T(2,128)(2,1)} %bitcast.9), calls=%async_computation.1 | async-start | bytes 2359296 | tf_op jit(solution)/shard_map/all_to_all | solution.py:129

commit v4 on v3

--- a/solution.py
+++ b/solution.py
@@ -11,6 +11,7 @@
 LMAX = 720
 EPS = 0.01
 LANES = 128
+VMEM_LIMIT = 24 * 2**20
 
 
 BITS = 7
@@ -33,9 +34,9 @@
     return cos_a * cos_b - sin_a * sin_b, sin_a * cos_b + cos_a * sin_b
 
 
-def fill_tables(step_cos_ref, step_sin_ref, cos_ref, sin_ref):
+def fill_tables(step_cos_ref, step_sin_ref, table_ref):
     step_cos, step_sin = step_cos_ref[...].T, step_sin_ref[...].T
-    slots, meridian_number = cos_ref.shape[1:]
+    slots, meridian_number = table_ref.shape[2:]
     lane = lax.broadcasted_iota(jnp.int32, (slots, LANES), 1)
     fine_cos = jnp.ones((slots, LANES), jnp.float32)
     fine_sin = jnp.zeros((slots, LANES), jnp.float32)
@@ -50,8 +51,8 @@
         column = slice(BITS + j, BITS + j + 1)
         cosine, sine = turn(fine_cos, fine_sin, step_cos[:, column], step_sin[:, column])
         at = slice(j * LANES, j * LANES + wide)
-        cos_ref[0, :, at] = cosine[:, :wide].astype(jnp.bfloat16)
-        sin_ref[0, :, at] = (-sine)[:, :wide].astype(jnp.bfloat16)
+        table_ref[0, 0, :, at] = cosine[:, :wide].astype(jnp.bfloat16)
+        table_ref[0, 1, :, at] = (-sine)[:, :wide].astype(jnp.bfloat16)
 
 
 def fill_tables_down(step_cos_ref, step_sin_ref, cos_ref, sin_ref):
@@ -90,35 +91,23 @@
         out_ref[:, part * width : (part + 1) * width] = (modes * live).astype(jnp.bfloat16)
 
 
-def inverse_kernel(zone_ref, back_ref, cos_ref, sin_ref, out_ref, total_ref):
-    slot = pl.program_id(0)
-    kinds, height, meridian_number = out_ref.shape
+def inverse_kernel(zone_ref, back_ref, table_ref, out_ref, flat_ref):
+    kinds, height, wide = out_ref.shape
     width = kinds * height
+    devices, length = back_ref.shape
     own_rows = zone_ref[lax.axis_index("lat")]
-    term = jnp.zeros((width, meridian_number), jnp.float32)
-    for part, table in enumerate((cos_ref, sin_ref)):
-        term = term + lax.dot_general(
-            back_ref[:, part * width : (part + 1) * width],
-            table[0],
-            (((0,), (0,)), ((), ())),
-            preferred_element_type=jnp.float32,
-        )
-
-    @pl.when(slot == 0)
+
+    @pl.when(pl.program_id(0) == 0)
     def _():
-        total_ref[...] = term
-
-    @pl.when(slot > 0)
-    def _():
-        total_ref[...] += term
-
-    @pl.when(slot == pl.num_programs(0) - 1)
-    def _():
-        place = lax.broadcasted_iota(jnp.int32, (height, meridian_number), 0)
-        live = (place < own_rows).astype(jnp.float32)
-        for kind in range(kinds):
-            rows = total_ref[kind * height : (kind + 1) * height, :]
-            out_ref[kind] = (rows * live).astype(jnp.bfloat16)
+        for piece in range(length // width):
+            block = back_ref[:, piece * width : (piece + 1) * width].astype(jnp.float32)
+            flat_ref[:, piece * devices : (piece + 1) * devices] = block.T.astype(jnp.bfloat16)
+
+    field = jnp.dot(flat_ref[...], table_ref[...], preferred_element_type=jnp.float32)
+    live = lax.broadcasted_iota(jnp.int32, (height, wide), 0) < own_rows
+    for kind in range(kinds):
+        rows = field[kind * height : (kind + 1) * height, :]
+        out_ref[kind] = (rows * live.astype(jnp.float32)).astype(jnp.bfloat16)
 
 
 def exchange(slabs):
@@ -154,16 +143,20 @@
                 ]
 
     poly = poly_ref[0]
-    coeffs = jnp.dot(modes_ref[...], poly, preferred_element_type=jnp.float32)
-    for tile in range(tiles):
-        coeff_ref[tile] = coeffs[:, tile * LANES : (tile + 1) * LANES]
+    modes = modes_ref[...]
+
+    def legendre(tile):
+        columns = poly[:, tile * LANES : (tile + 2) * LANES]
+        coeffs = jnp.dot(modes, columns, preferred_element_type=jnp.float32)
+        coeff_ref[tile] = coeffs[:, :LANES]
+        coeff_ref[tile + 1] = coeffs[:, LANES:]
 
     def per_tile(tile, carry):
         real = [coeff_ref[tile, pl.ds(m, kinds, stride=members), :] for m in range(members)]
         imag = [coeff_ref[tile, pl.ds(half + m, kinds, stride=members), :] for m in range(members)]
         pair_real = [jnp.zeros_like(real[0]) for _ in range(members)]
         pair_imag = [jnp.zeros_like(real[0]) for _ in range(members)]
-        lanes = pl.ds(pl.multiple_of(tile * LANES, LANES), LANES)
+        lanes = slice(tile * LANES, (tile + 1) * LANES)
         truth_real, truth_imag = truth_ref[0, 0, :, lanes], truth_ref[0, 1, :, lanes]
         weight = weight_ref[0, :, lanes]
         for m in range(members):
@@ -182,16 +175,17 @@
             )
         return carry
 
-    lax.fori_loop(0, tiles, per_tile, 0)
-
-    back = jnp.zeros(modes_ref.shape, jnp.float32)
-    for tile in range(tiles):
-        back = back + lax.dot_general(
-            coeff_ref[tile].astype(jnp.bfloat16),
-            poly[:, tile * LANES : (tile + 1) * LANES],
-            (((1,), (1,)), ((), ())),
-            preferred_element_type=jnp.float32,
-        )
+    legendre(0)
+    for tile in range(0, tiles, 2):
+        if tile + 2 < tiles:
+            legendre(tile + 2)
+        per_tile(tile, 0)
+        per_tile(tile + 1, 0)
+
+    grads = jnp.concatenate([coeff_ref[tile].astype(jnp.bfloat16) for tile in range(tiles)], axis=1)
+    back = lax.dot_general(
+        grads, poly, (((1,), (1,)), ((), ())), preferred_element_type=jnp.float32
+    )
     modes_ref[...] = back.astype(jnp.bfloat16)
 
     for band in range(bands):
@@ -222,8 +216,6 @@
     orders = order_of_place.reshape(devices, slot_dev).T.reshape(slots)
     step_cos, step_sin = angle_tables(orders, meridian_number)
     step_spec = pl.BlockSpec((step_cos.shape[0], devices), lambda s: (0, s))
-    table_spec = pl.BlockSpec((1, devices, meridian_number), lambda s: (s, 0, 0))
-    table_shape = jax.ShapeDtypeStruct((slot_dev, devices, meridian_number), jnp.bfloat16)
     scalars = pl.BlockSpec(memory_space=pltpu.SMEM)
     exchange_shape = jax.ShapeDtypeStruct((devices, slot_dev * 2 * width), jnp.bfloat16)
     slab = pl.BlockSpec((devices, 2 * width), lambda s: (0, s))
@@ -236,15 +228,16 @@
         out_specs=slab,
         out_shape=exchange_shape,
         scratch_shapes=[pltpu.VMEM((meridian_number, devices), jnp.bfloat16)] * 2,
+        compiler_params=pltpu.CompilerParams(vmem_limit_bytes=VMEM_LIMIT),
         name="forward_dft",
     )(parallels_in_zone, predicted_fields[0], step_cos, step_sin)
     modes, step_cos, step_sin = lax.optimization_barrier((modes, step_cos, step_sin))
-    table_cos, table_sin = pl.pallas_call(
+    table = pl.pallas_call(
         fill_tables,
         grid=(slot_dev,),
         in_specs=[step_spec, step_spec],
-        out_specs=[table_spec, table_spec],
-        out_shape=[table_shape, table_shape],
+        out_specs=pl.BlockSpec((1, 2, devices, meridian_number), lambda s: (s, 0, 0, 0)),
+        out_shape=jax.ShapeDtypeStruct((slot_dev, 2, devices, meridian_number), jnp.bfloat16),
         cost_estimate=pl.CostEstimate(
             flops=8 * slots * meridian_number,
             bytes_accessed=4 * slots * meridian_number,
@@ -277,19 +270,26 @@
             pltpu.VMEM((2 * kinds * members, places), jnp.bfloat16),
             pltpu.VMEM((degrees // LANES, 2 * kinds * members, LANES), jnp.float32),
         ],
+        compiler_params=pltpu.CompilerParams(vmem_limit_bytes=VMEM_LIMIT),
         name="score_gradient",
     )(gathered, weighted_polynomial, truth_spectrum, weight)
     returned = exchange(back)
 
+    wide = 3 * LANES
     field = pl.pallas_call(
         inverse_kernel,
-        grid=(slot_dev,),
-        in_specs=[scalars, slab, table_spec, table_spec],
-        out_specs=whole,
+        grid=(pl.cdiv(meridian_number, wide),),
+        in_specs=[
+            scalars,
+            pl.BlockSpec((devices, slot_dev * 2 * width), lambda n: (0, 0)),
+            pl.BlockSpec((2 * slots, wide), lambda n: (0, n)),
+        ],
+        out_specs=pl.BlockSpec((kinds, height, wide), lambda n: (0, 0, n)),
         out_shape=jax.ShapeDtypeStruct((kinds, height, meridian_number), jnp.bfloat16),
-        scratch_shapes=[pltpu.VMEM((width, meridian_number), jnp.float32)],
+        scratch_shapes=[pltpu.VMEM((width, 2 * slots), jnp.bfloat16)],
+        compiler_params=pltpu.CompilerParams(vmem_limit_bytes=59 * 2**20),
         name="inverse_dft",
-    )(parallels_in_zone, returned, table_cos, table_sin)
+    )(parallels_in_zone, returned, table.reshape(2 * slots, meridian_number))
     return field[None]
 
 

time: 129 us -> 122 us (0.946)
  Pallas kernels: 33.7 us -> 27.6 us
    pallas_call x1, Pallas kernels: 15.3 us -> 10.2 us  [local(): pl.pallas_call(functools.partial(score_kernel, bands, members, kinds, hei...]
    transpose x2, local copies, waits for them, and re-layouts: 6.39 us -> 3.85 us  [exchange(): pieces = halves.transpose(0, 2, 1, 3).reshape(devices, 2, length // 2)]
    unnamed x4 -> x18, local copies, waits for them, and re-layouts: 2.35 us -> 4.64 us
    pallas_call x1, Pallas kernels: 5.71 us -> 4.22 us  [local(): pl.pallas_call(forward_kernel, grid=(slot_dev,), in_specs=[scalars, whole...]
where the time goes in v4:
time: 122 us; the launch traced here: 121 us
  waiting for transfers between devices  60.4 us (50%)
  Pallas kernels  27.6 us (23%)
  starting transfers between devices  21.7 us (18%)
  local copies, waits for them, and re-layouts  10.2 us (8%)
    all_to_all x2, waiting for transfers between devices, exchange(): lax.all_to_all(pieces, ('lat', 'mem'), split_axis=0, concat_axis=0, tiled...  60.4 us
    all_to_all x2, starting transfers between devices, exchange(): lax.all_to_all(pieces, ('lat', 'mem'), split_axis=0, concat_axis=0, tiled...  21.7 us
    pallas_call x1, Pallas kernels, local(): pl.pallas_call(functools.partial(score_kernel, bands, members, kinds, hei...  10.2 us
    pallas_call x1, Pallas kernels, local(): pl.pallas_call(inverse_kernel, grid=(pl.cdiv(meridian_number, wide),), in...  6.62 us
    pallas_call x1, Pallas kernels, local(): pl.pallas_call(fill_tables, grid=(slot_dev,), in_specs=[step_spec, step_s...  6.61 us
    unnamed x18, local copies, waits for them, and re-layouts  4.64 us
    pallas_call x1, Pallas kernels, local(): pl.pallas_call(forward_kernel, grid=(slot_dev,), in_specs=[scalars, whole...  4.22 us
    transpose x2, local copies, waits for them, and re-layouts, exchange(): pieces = halves.transpose(0, 2, 1, 3).reshape(devices, 2, length // 2)  3.85 us
  transfers between devices with their start and end apart: 2, of which 2 were waited for; matrix products, arithmetic and copies ran while one was open for 1% of the time, Pallas kernels for 5%

profile of v4, /device:TPU:1, one launch (start us, length us, event | category | flops | bytes accessed | tf_op | source)
XLA Modules:
  0.0 121.3 jit_solution(14735548631529526291)
XLA Ops:
  0.0 0.9 reshape.89
  0.9 0.1 copy.9
  1.0 0.4 select_multiply_fusion
  1.4 0.0 copy-start.2
  1.4 0.0 copy-start.3
  1.4 0.0 copy-start.1
  1.4 1.3 %copy-done.1 = bf16[1,8,48,1440]{3,2,1,0:T(8,128)(2,1)S(1)} copy-done((bf16[1,8,48,1440]{3,2,1,0:T(8,128)(2,1)S(1)}, bf16[1,8,48,1440]{3,2,1,0:T(8,128)(2,1)}, u32[]{:S(2)}) %copy-start.1) | copy-done | bytes 1105944
  2.8 0.0 copy-start.6
  2.8 0.7 copy-done.6
  3.4 4.2 %forward_dft.1 = bf16[256,2304]{1,0:T(8,128)(2,1)S(1)} custom-call(s32[16]{0:T(128)S(1)} %copy-done.6, bf16[8,48,1440]{2,1,0:T(8,128)(2,1)S(1)} %bitcast.21, f32[24,768]{1,0:T(8,128)S(1)} %get-tuple-element.9.step_cos_ref, f32[24,768]{1,0:T(8,128)S(1)} %get-tuple-element.10.step_sin_ref), custom_call_target="tpu_custom_call" | custom-call | tf_op jit(solution)/shard_map/forward_dft/pallas_call | solution.py:224
  7.6 0.0 copy-done.2
  7.6 0.0 copy-done.3
  7.7 0.0 copy-start.7
  7.7 1.9 %copy.10 = bf16[32,8,2,1152]{3,2,1,0:T(2,128)(2,1)} copy(bf16[32,8,2,1152]{3,1,2,0:T(8,128)(2,1)S(1)} %bitcast.18) | data formatting | bytes 2359296 | tf_op jit(solution)/shard_map/transpose | solution.py:117
  9.6 0.0 copy-start
  9.6 16.5 %all-to-all-start = ((bf16[256,2,1152]{2,1,0:T(2,128)(2,1)}), bf16[256,2,1152]{2,1,0:T(2,128)(2,1)}, u32[]{:S(2)}, u32[]{:S(2)}) async-start(bf16[256,2,1152]{2,1,0:T(2,128)(2,1)} %bitcast.24), calls=%async_computation | async-start | bytes 2359296 | tf_op jit(solution)/shard_map/all_to_all | solution.py:118
  26.1 0.8 dynamic_slice.3
  26.9 0.1 fusion.6
  27.0 0.0 copy-done.7
  27.0 0.7 broadcast_multiply_fusion.weight_ref
  27.7 32.4 %all-to-all-done = bf16[256,2,1152]{2,1,0:T(2,128)(2,1)} async-done(((bf16[256,2,1152]{2,1,0:T(2,128)(2,1)}), bf16[256,2,1152]{2,1,0:T(2,128)(2,1)}, u32[]{:S(2)}, u32[]{:S(2)}) %all-to-all-start) | async-done | bytes 1179680 | tf_op jit(solution)/shard_map/all_to_all | solution.py:118
  60.1 1.4 %copy.12 = bf16[32,8,2,1152]{3,1,2,0:T(8,128)(2,1)S(1)} copy(bf16[32,8,2,1152]{3,2,1,0:T(2,128)(2,1)} %bitcast.14) | data formatting | bytes 2359296
  61.6 0.0 copy-done
  61.6 0.0 copy-done.4
  61.6 0.0 copy-done.5
  61.6 10.2 %score_gradient.1 = bf16[256,2304]{1,0:T(8,128)(2,1)S(1)} custom-call(bf16[256,2304]{1,0:T(8,128)(2,1)S(1)} %bitcast.19, bf16[3,768,768]{2,1,0:T(8,128)(2,1)S(1)} %copy-done, f32[3,2,8,768]{3,2,1,0:T(8,128)S(1)} %copy-done.5, f32[3,8,768]{2,1,0:T(8,128)S(1)} %copy-done.4), custom_call_target="tpu_custom_call" | custom-call | tf_op jit(solution)/shard_map/score_gradient/pallas_call | solution.py:258
  71.8 1.9 %copy.11 = bf16[32,8,2,1152]{3,2,1,0:T(2,128)(2,1)} copy(bf16[32,8,2,1152]{3,1,2,0:T(8,128)(2,1)S(1)} %bitcast.20) | data formatting | bytes 2359296 | tf_op jit(solution)/shard_map/transpose | solution.py:117
  73.7 5.2 %all-to-all-start.1 = ((bf16[256,2,1152]{2,1,0:T(2,128)(2,1)}), bf16[256,2,1152]{2,1,0:T(2,128)(2,1)S(1)}, u32[]{:S(2)}, u32[]{:S(2)}) async-start(bf16[256,2,1152]{2,1,0:T(2,128)(2,1)} %bitcast.9), calls=%async_computation.1 | async-start | bytes 2359296 | tf_op jit(solution)/shard_map/all_to_all | solution.py:118
  78.9 6.6 %inverse_tables.1 = bf16[3,2,256,1440]{3,2,1,0:T(8,128)(2,1)} custom-call(f32[24,768]{1,0:T(8,128)} %copy-done.3, f32[24,768]{1,0:T(8,128)} %copy-done.2), custom_call_target="tpu_custom_call" | custom-call | flops 8847360 | bytes 4423680 | tf_op jit(solution)/shard_map/inverse_tables/pallas_call | solution.py:235
  85.5 28.0 %all-to-all-done.1 = bf16[256,2,1152]{2,1,0:T(2,128)(2,1)S(1)} async-done(((bf16[256,2,1152]{2,1,0:T(2,128)(2,1)}), bf16[256,2,1152]{2,1,0:T(2,128)(2,1)S(1)}, u32[]{:S(2)}, u32[]{:S(2)}) %all-to-all-start.1) | async-done | bytes 1179680 | tf_op jit(solution)/shard_map/all_to_all | solution.py:118
  113.5 1.2 copy.13
  114.7 6.6 %inverse_dft.1 = bf16[8,48,1440]{2,1,0:T(8,128)(2,1)} custom-call(s32[16]{0:T(128)} %zone_ref.3, bf16[256,2304]{1,0:T(8,128)(2,1)} %bitcast.23, bf16[1536,1440]{1,0:T(8,128)(2,1)} %bitcast.22), custom_call_target="tpu_custom_call" | custom-call | tf_op jit(solution)/shard_map/inverse_dft/pallas_call | solution.py:279
  (7 shorter events, 0.0 us)
Async XLA Ops:
  1.4 6.2 %copy-start.2 = (f32[24,768]{1,0:T(8,128)}, f32[24,768]{1,0:T(8,128)S(1)}, u32[]{:S(2)}) copy-start(f32[24,768]{1,0:T(8,128)S(1)} %get-tuple-element.10.step_sin_ref) | copy-start | bytes 221188
  1.4 6.2 %copy-start.3 = (f32[24,768]{1,0:T(8,128)}, f32[24,768]{1,0:T(8,128)S(1)}, u32[]{:S(2)}) copy-start(f32[24,768]{1,0:T(8,128)S(1)} %get-tuple-element.9.step_cos_ref) | copy-start | bytes 221188
  1.4 1.3 %copy-start.1 = (bf16[1,8,48,1440]{3,2,1,0:T(8,128)(2,1)S(1)}, bf16[1,8,48,1440]{3,2,1,0:T(8,128)(2,1)}, u32[]{:S(2)}) copy-start(bf16[1,8,48,1440]{3,2,1,0:T(8,128)(2,1)} %param.6) | copy-start | bytes 3317764
  2.8 0.7 copy-start.6
  7.7 19.3 %copy-start.7 = (f32[8]{0:T(128)S(1)}, f32[8]{0:T(128)}, u32[]{:S(2)}) copy-start(f32[8]{0:T(128)} %param.9) | copy-start | bytes 100
  9.6 52.0 %copy-start = (bf16[3,768,768]{2,1,0:T(8,128)(2,1)S(1)}, bf16[3,768,768]{2,1,0:T(8,128)(2,1)}, u32[]{:S(2)}) copy-start(bf16[3,768,768]{2,1,0:T(8,128)(2,1)} %poly_ref.1) | copy-start | bytes 10616836
  9.6 50.5 %all-to-all-start = ((bf16[256,2,1152]{2,1,0:T(2,128)(2,1)}), bf16[256,2,1152]{2,1,0:T(2,128)(2,1)}, u32[]{:S(2)}, u32[]{:S(2)}) async-start(bf16[256,2,1152]{2,1,0:T(2,128)(2,1)} %bitcast.24), calls=%async_computation | async-start | bytes 2359296 | tf_op jit(solution)/shard_map/all_to_all | solution.py:118
  60.1 1.5 %copy-start.4 = (f32[3,8,768]{2,1,0:T(8,128)S(1)}, f32[3,8,768]{2,1,0:T(8,128)}, u32[]{:S(2)}) copy-start(f32[3,8,768]{2,1,0:T(8,128)} %broadcast_multiply_fusion.weight_ref) | copy-start | bytes 221188
  60.1 1.5 %copy-start.5 = (f32[3,2,8,768]{3,2,1,0:T(8,128)S(1)}, f32[3,2,8,768]{3,2,1,0:T(8,128)}, u32[]{:S(2)}) copy-start(f32[3,2,8,768]{3,2,1,0:T(8,128)} %truth_ref.1) | copy-start | bytes 442372
  73.7 39.8 %all-to-all-start.1 = ((bf16[256,2,1152]{2,1,0:T(2,128)(2,1)}), bf16[256,2,1152]{2,1,0:T(2,128)(2,1)S(1)}, u32[]{:S(2)}, u32[]{:S(2)}) async-start(bf16[256,2,1152]{2,1,0:T(2,128)(2,1)} %bitcast.9), calls=%async_computation.1 | async-start | bytes 2359296 | tf_op jit(solution)/shard_map/all_to_all | solution.py:118

commit v5 on v4

--- a/solution.py
+++ b/solution.py
@@ -275,7 +275,7 @@
     )(gathered, weighted_polynomial, truth_spectrum, weight)
     returned = exchange(back)
 
-    wide = 3 * LANES
+    wide = 4 * LANES
     field = pl.pallas_call(
         inverse_kernel,
         grid=(pl.cdiv(meridian_number, wide),),

time: 122 us -> 121 us (level)
  no operation moved by 1% of the time
where the time goes in v5:
time: 121 us
  waiting for transfers between devices  60.4 us (50%)
  Pallas kernels  27.1 us (22%)
  starting transfers between devices  21.7 us (18%)
  local copies, waits for them, and re-layouts  10.2 us (8%)
  other arithmetic  1.21 us (1%)
    all_to_all x2, waiting for transfers between devices, exchange(): lax.all_to_all(pieces, ('lat', 'mem'), split_axis=0, concat_axis=0, tiled...  60.4 us
    all_to_all x2, starting transfers between devices, exchange(): lax.all_to_all(pieces, ('lat', 'mem'), split_axis=0, concat_axis=0, tiled...  21.7 us
    pallas_call x1, Pallas kernels, local(): pl.pallas_call(functools.partial(score_kernel, bands, members, kinds, hei...  10.2 us
    pallas_call x1, Pallas kernels, local(): pl.pallas_call(fill_tables, grid=(slot_dev,), in_specs=[step_spec, step_s...  6.61 us
    pallas_call x1, Pallas kernels, local(): pl.pallas_call(inverse_kernel, grid=(pl.cdiv(meridian_number, wide),), in...  6.03 us
    unnamed x18, local copies, waits for them, and re-layouts  4.64 us
    pallas_call x1, Pallas kernels, local(): pl.pallas_call(forward_kernel, grid=(slot_dev,), in_specs=[scalars, whole...  4.22 us
    transpose x2, local copies, waits for them, and re-layouts, exchange(): pieces = halves.transpose(0, 2, 1, 3).reshape(devices, 2, length // 2)  3.85 us
  transfers between devices with their start and end apart: 2, of which 2 were waited for; matrix products, arithmetic and copies ran while one was open for 1% of the time, Pallas kernels for 5%

profile of v5, /device:TPU:1, one launch (start us, length us, event | category | flops | bytes accessed | tf_op | source)
XLA Modules:
  0.0 120.8 jit_solution(13117610937549122072)
XLA Ops:
  0.0 0.9 reshape.89
  0.9 0.1 copy.9
  1.0 0.4 select_multiply_fusion
  1.4 0.0 copy-start.2
  1.4 0.0 copy-start.3
  1.4 0.0 copy-start.1
  1.4 1.3 %copy-done.1 = bf16[1,8,48,1440]{3,2,1,0:T(8,128)(2,1)S(1)} copy-done((bf16[1,8,48,1440]{3,2,1,0:T(8,128)(2,1)S(1)}, bf16[1,8,48,1440]{3,2,1,0:T(8,128)(2,1)}, u32[]{:S(2)}) %copy-start.1) | copy-done | bytes 1105944
  2.8 0.0 copy-start.6
  2.8 0.7 copy-done.6
  3.4 4.2 %forward_dft.1 = bf16[256,2304]{1,0:T(8,128)(2,1)S(1)} custom-call(s32[16]{0:T(128)S(1)} %copy-done.6, bf16[8,48,1440]{2,1,0:T(8,128)(2,1)S(1)} %bitcast.21, f32[24,768]{1,0:T(8,128)S(1)} %get-tuple-element.9.step_cos_ref, f32[24,768]{1,0:T(8,128)S(1)} %get-tuple-element.10.step_sin_ref), custom_call_target="tpu_custom_call" | custom-call | tf_op jit(solution)/shard_map/forward_dft/pallas_call | solution.py:224
  7.6 0.0 copy-done.2
  7.6 0.0 copy-done.3
  7.7 0.0 copy-start.7
  7.7 1.9 %copy.10 = bf16[32,8,2,1152]{3,2,1,0:T(2,128)(2,1)} copy(bf16[32,8,2,1152]{3,1,2,0:T(8,128)(2,1)S(1)} %bitcast.18) | data formatting | bytes 2359296 | tf_op jit(solution)/shard_map/transpose | solution.py:117
  9.6 0.0 copy-start
  9.6 16.5 %all-to-all-start = ((bf16[256,2,1152]{2,1,0:T(2,128)(2,1)}), bf16[256,2,1152]{2,1,0:T(2,128)(2,1)}, u32[]{:S(2)}, u32[]{:S(2)}) async-start(bf16[256,2,1152]{2,1,0:T(2,128)(2,1)} %bitcast.24), calls=%async_computation | async-start | bytes 2359296 | tf_op jit(solution)/shard_map/all_to_all | solution.py:118
  26.1 0.8 dynamic_slice.3
  26.9 0.1 fusion.6
  27.0 0.0 copy-done.7
  27.0 0.7 broadcast_multiply_fusion.weight_ref
  27.7 32.4 %all-to-all-done = bf16[256,2,1152]{2,1,0:T(2,128)(2,1)} async-done(((bf16[256,2,1152]{2,1,0:T(2,128)(2,1)}), bf16[256,2,1152]{2,1,0:T(2,128)(2,1)}, u32[]{:S(2)}, u32[]{:S(2)}) %all-to-all-start) | async-done | bytes 1179680 | tf_op jit(solution)/shard_map/all_to_all | solution.py:118
  60.1 1.4 %copy.12 = bf16[32,8,2,1152]{3,1,2,0:T(8,128)(2,1)S(1)} copy(bf16[32,8,2,1152]{3,2,1,0:T(2,128)(2,1)} %bitcast.14) | data formatting | bytes 2359296
  61.6 0.0 copy-done
  61.6 0.0 copy-done.4
  61.6 0.0 copy-done.5
  61.6 10.2 %score_gradient.1 = bf16[256,2304]{1,0:T(8,128)(2,1)S(1)} custom-call(bf16[256,2304]{1,0:T(8,128)(2,1)S(1)} %bitcast.19, bf16[3,768,768]{2,1,0:T(8,128)(2,1)S(1)} %copy-done, f32[3,2,8,768]{3,2,1,0:T(8,128)S(1)} %copy-done.5, f32[3,8,768]{2,1,0:T(8,128)S(1)} %copy-done.4), custom_call_target="tpu_custom_call" | custom-call | tf_op jit(solution)/shard_map/score_gradient/pallas_call | solution.py:258
  71.8 1.9 %copy.11 = bf16[32,8,2,1152]{3,2,1,0:T(2,128)(2,1)} copy(bf16[32,8,2,1152]{3,1,2,0:T(8,128)(2,1)S(1)} %bitcast.20) | data formatting | bytes 2359296 | tf_op jit(solution)/shard_map/transpose | solution.py:117
  73.7 5.2 %all-to-all-start.1 = ((bf16[256,2,1152]{2,1,0:T(2,128)(2,1)}), bf16[256,2,1152]{2,1,0:T(2,128)(2,1)S(1)}, u32[]{:S(2)}, u32[]{:S(2)}) async-start(bf16[256,2,1152]{2,1,0:T(2,128)(2,1)} %bitcast.9), calls=%async_computation.1 | async-start | bytes 2359296 | tf_op jit(solution)/shard_map/all_to_all | solution.py:118
  78.9 6.6 %inverse_tables.1 = bf16[3,2,256,1440]{3,2,1,0:T(8,128)(2,1)} custom-call(f32[24,768]{1,0:T(8,128)} %copy-done.3, f32[24,768]{1,0:T(8,128)} %copy-done.2), custom_call_target="tpu_custom_call" | custom-call | flops 8847360 | bytes 4423680 | tf_op jit(solution)/shard_map/inverse_tables/pallas_call | solution.py:235
  85.5 28.0 %all-to-all-done.1 = bf16[256,2,1152]{2,1,0:T(2,128)(2,1)S(1)} async-done(((bf16[256,2,1152]{2,1,0:T(2,128)(2,1)}), bf16[256,2,1152]{2,1,0:T(2,128)(2,1)S(1)}, u32[]{:S(2)}, u32[]{:S(2)}) %all-to-all-start.1) | async-done | bytes 1179680 | tf_op jit(solution)/shard_map/all_to_all | solution.py:118
  113.5 1.2 copy.13
  114.7 6.0 %inverse_dft.1 = bf16[8,48,1440]{2,1,0:T(8,128)(2,1)} custom-call(s32[16]{0:T(128)} %zone_ref.3, bf16[256,2304]{1,0:T(8,128)(2,1)} %bitcast.23, bf16[1536,1440]{1,0:T(8,128)(2,1)} %bitcast.22), custom_call_target="tpu_custom_call" | custom-call | tf_op jit(solution)/shard_map/inverse_dft/pallas_call | solution.py:279
  (7 shorter events, 0.0 us)
Async XLA Ops:
  1.4 6.2 %copy-start.2 = (f32[24,768]{1,0:T(8,128)}, f32[24,768]{1,0:T(8,128)S(1)}, u32[]{:S(2)}) copy-start(f32[24,768]{1,0:T(8,128)S(1)} %get-tuple-element.10.step_sin_ref) | copy-start | bytes 221188
  1.4 6.2 %copy-start.3 = (f32[24,768]{1,0:T(8,128)}, f32[24,768]{1,0:T(8,128)S(1)}, u32[]{:S(2)}) copy-start(f32[24,768]{1,0:T(8,128)S(1)} %get-tuple-element.9.step_cos_ref) | copy-start | bytes 221188
  1.4 1.3 %copy-start.1 = (bf16[1,8,48,1440]{3,2,1,0:T(8,128)(2,1)S(1)}, bf16[1,8,48,1440]{3,2,1,0:T(8,128)(2,1)}, u32[]{:S(2)}) copy-start(bf16[1,8,48,1440]{3,2,1,0:T(8,128)(2,1)} %param.6) | copy-start | bytes 3317764
  2.8 0.7 copy-start.6
  7.7 19.3 %copy-start.7 = (f32[8]{0:T(128)S(1)}, f32[8]{0:T(128)}, u32[]{:S(2)}) copy-start(f32[8]{0:T(128)} %param.9) | copy-start | bytes 100
  9.6 52.0 %copy-start = (bf16[3,768,768]{2,1,0:T(8,128)(2,1)S(1)}, bf16[3,768,768]{2,1,0:T(8,128)(2,1)}, u32[]{:S(2)}) copy-start(bf16[3,768,768]{2,1,0:T(8,128)(2,1)} %poly_ref.1) | copy-start | bytes 10616836
  9.6 50.5 %all-to-all-start = ((bf16[256,2,1152]{2,1,0:T(2,128)(2,1)}), bf16[256,2,1152]{2,1,0:T(2,128)(2,1)}, u32[]{:S(2)}, u32[]{:S(2)}) async-start(bf16[256,2,1152]{2,1,0:T(2,128)(2,1)} %bitcast.24), calls=%async_computation | async-start | bytes 2359296 | tf_op jit(solution)/shard_map/all_to_all | solution.py:118
  60.1 1.5 %copy-start.4 = (f32[3,8,768]{2,1,0:T(8,128)S(1)}, f32[3,8,768]{2,1,0:T(8,128)}, u32[]{:S(2)}) copy-start(f32[3,8,768]{2,1,0:T(8,128)} %broadcast_multiply_fusion.weight_ref) | copy-start | bytes 221188
  60.1 1.5 %copy-start.5 = (f32[3,2,8,768]{3,2,1,0:T(8,128)S(1)}, f32[3,2,8,768]{3,2,1,0:T(8,128)}, u32[]{:S(2)}) copy-start(f32[3,2,8,768]{3,2,1,0:T(8,128)} %truth_ref.1) | copy-start | bytes 442372
  73.7 39.8 %all-to-all-start.1 = ((bf16[256,2,1152]{2,1,0:T(2,128)(2,1)}), bf16[256,2,1152]{2,1,0:T(2,128)(2,1)S(1)}, u32[]{:S(2)}, u32[]{:S(2)}) async-start(bf16[256,2,1152]{2,1,0:T(2,128)(2,1)} %bitcast.9), calls=%async_computation.1 | async-start | bytes 2359296 | tf_op jit(solution)/shard_map/all_to_all | solution.py:118
